TPU v7x, 768 devices: a whole 4x8x12 slice. The times are simulated.
768 devices in a mesh: axial: 96 (over x, z, y_lo), azim: 8 (over y_hi, core).
Axes of the slice: x: 4, y: 8 (y_hi: 4, y_lo: 2; y = y_hi * 2 + y_lo), z: 12, core: 2. Of those that a mesh axis runs over, the one named last changes fastest.
Arguments:
- source: float32 [12, 384, 128, 256], P(None, 'axial', 'azim'), may hold values from -24 to 24
- storage: float32 [12, 384, 128, 256], P(None, 'axial', 'azim'), may hold values from 0.5 to 2
- materials: int32 [384, 128, 256], P('axial', 'azim'), may hold values from 0 to 3
- conductance: float32 [12], replicated, may hold values from 0.3 to 2
- mixing: float32 [4, 12, 12], replicated, may hold values from -0.9 to 0.9
- counts: int32 [96, 8], P('axial', 'azim'), may hold values from 30 to 120, as said below
- vis_owner: int32 [96, 8, 120, 4], P('axial', 'azim'), may hold values from 0 to 95, as said below
- vis_slot: int32 [96, 8, 120, 4], P('axial', 'azim'), may hold values from 0 to 119, as said below
- vis_block: int32 [96, 8, 120, 4], P('axial', 'azim'), may hold values from 0 to 7
- radiosity_old: bfloat16 [96, 8, 120, 128], P('axial', 'azim'), may hold values from -6 to 6
- view_blocks: bfloat16 [8, 128, 128], replicated, may hold values from -0.25 to 0.25
- emission: float32 [96, 8, 120, 128], P('axial', 'azim'), may hold values from 0.5 to 1.5
- reflect: float32 [96, 8, 120, 128], P('axial', 'azim'), may hold values from 0.2 to 0.8
Outputs:
- solution: float32 [12, 384, 128, 256], P(None, 'axial', 'azim')
- residual: float32 [12, 384, 128, 256], P(None, 'axial', 'azim')
- radiosity_new: float32 [96, 8, 120, 128], P('axial', 'azim')
Inputs may be any that keep to these rules, and one draw needn't show every extreme that they name: Slots 0 to counts - 1 of a device hold its panels; some device has exactly 120. `vis_owner`: owners lie in the same azimuthal column as the panel. Among the entries of the live panels of one device, no owner is named more than 5 times; some device names every owner exactly 5 times, and some owner is named exactly 5 times by every device. `vis_slot`: every entry is below the count of the named owner in the same azimuthal column.
All inputs are finite; a program needn't handle non-finite values.
Results may differ from a plain program's by a relative error of at most 0.0004.
Values may be sent and summed in bfloat16 or wider, within the bound.
A program may use at most 128 MiB of HBM per device.

v0:
```python
import jax
import jax.numpy as jnp
from jax import lax
from jax.sharding import PartitionSpec as P

ITERS = 3


center_value = 14.2
half_width = 13.8


def extended(cells, sides, width, closed):
    for axis, dim in sides:
        count = lax.axis_size(axis)
        ends = count if closed else count - 1
        head = lax.slice_in_dim(cells, 0, width, axis=dim)
        tail = lax.slice_in_dim(cells, cells.shape[dim] - width, cells.shape[dim], axis=dim)
        cells = jnp.concatenate(
            [
                lax.ppermute(tail, axis, [(i, (i + 1) % count) for i in range(ends)]),
                cells,
                lax.ppermute(head, axis, [((i + 1) % count, i) for i in range(ends)]),
            ],
            axis=dim,
        )
    return cells


def combine(field, axial_ext, azim_ext, storage, masks, mixing, conductance):
    radial_pad = jnp.pad(field, ((0, 0), (0, 0), (0, 0), (1, 1)))
    beside = axial_ext[:, 2:] + axial_ext[:, :-2] + azim_ext[:, :, 2:] + azim_ext[:, :, :-2]
    beside = beside + radial_pad[..., 2:] + radial_pad[..., :-2]
    weighted = masks[:, None] * field[None]
    mixed = jnp.einsum("mfg,mgazr->fazr", mixing, weighted, precision=lax.Precision.HIGHEST)
    return storage * field + mixed + conductance[:, None, None, None] * (6.0 * field - beside)


def chebyshev(source, operator_fn):
    spread_ratio = center_value / half_width
    ratio_now = 1.0 / spread_ratio
    solution = jnp.zeros_like(source)
    residual = source
    direction = source / center_value
    for iteration in range(ITERS):
        solution = solution + direction
        residual = residual - operator_fn(direction)
        if iteration + 1 < ITERS:
            ratio_next = 1.0 / (2.0 * spread_ratio - ratio_now)
            direction = (
                ratio_next * ratio_now * direction + 2.0 * ratio_next / half_width * residual
            )
            ratio_now = ratio_next
    return (solution, residual)


def body(
    source,
    storage,
    materials,
    conductance,
    mixing,
    counts,
    vis_owner,
    vis_slot,
    vis_block,
    radiosity_old,
    view_blocks,
    emission,
    reflect,
):
    kinds = mixing.shape[0]
    masks = (materials[None] == jnp.arange(kinds, dtype=jnp.int32)[:, None, None, None]).astype(
        jnp.float32
    )

    def operator_step(direction):
        axial_ext = extended(direction, (("axial", 1),), 1, False)
        azim_ext = extended(direction, (("azim", 2),), 1, True)
        return combine(direction, axial_ext, azim_ext, storage, masks, mixing, conductance)

    solution, residual = chebyshev(source, operator_step)
    slot_count = vis_owner.shape[2]
    visible = vis_owner.shape[3]
    values = radiosity_old.shape[3]
    requests_total = slot_count * visible
    live_count = counts[0, 0]
    owner_flat = vis_owner.reshape(requests_total)
    slot_flat = vis_slot.reshape(requests_total)
    live = jnp.arange(requests_total, dtype=jnp.int32) < visible * live_count
    owners_total = lax.axis_size("axial")
    local_panels = radiosity_old[0, 0]
    cap_slots = requests_total // owners_total
    hits = (
        (owner_flat[:, None] == jnp.arange(owners_total, dtype=jnp.int32)[None, :]) & live[:, None]
    ).astype(jnp.int32)
    earlier = jnp.cumsum(hits, axis=0) - hits
    rank = jnp.sum(earlier * hits, axis=1)
    target = jnp.where(live, owner_flat, owners_total)
    asked = (
        jnp.full((owners_total, cap_slots), -1, jnp.int32)
        .at[target, rank]
        .set(slot_flat, mode="drop")
    )
    requested = lax.all_to_all(asked, "axial", split_axis=0, concat_axis=0, tiled=True)
    rows_out = local_panels[jnp.clip(requested, 0)]
    rows_out = jnp.where(requested[..., None] >= 0, rows_out, jnp.zeros_like(rows_out))
    returned = lax.all_to_all(rows_out, "axial", split_axis=0, concat_axis=0, tiled=True)
    flat_rows = returned.reshape(owners_total * cap_slots, values)
    picked = flat_rows[jnp.where(live, owner_flat * cap_slots + rank, 0)]
    gathered = jnp.where(live[:, None], picked.astype(jnp.float32), 0.0)
    block_types = view_blocks.shape[0]
    block_hot = (
        (
            vis_block.reshape(requests_total)[:, None]
            == jnp.arange(block_types, dtype=jnp.int32)[None, :]
        )
        & live[:, None]
    ).astype(jnp.float32)
    grouped = jnp.einsum(
        "pkb,pkr->bpr",
        block_hot.reshape(slot_count, visible, block_types),
        gathered.reshape(slot_count, visible, values),
        precision=lax.Precision.HIGHEST,
    )
    incoming = jnp.einsum(
        "bij,bpj->pi", view_blocks.astype(jnp.float32), grouped, precision=lax.Precision.HIGHEST
    )
    wall = solution[0, :, :, -1].reshape(-1)
    wall_temp = wall[jnp.arange(slot_count, dtype=jnp.int32) % wall.shape[0]]
    panel_live = jnp.arange(slot_count, dtype=jnp.int32) < live_count
    radiosity_new = jnp.where(
        panel_live[:, None], emission[0, 0] * wall_temp[:, None] + reflect[0, 0] * incoming, 0.0
    )
    return (solution, residual, radiosity_new[None, None])


def solution(mesh):
    return jax.shard_map(
        body,
        mesh=mesh,
        in_specs=(
            P(None, "axial", "azim", None),
            P(None, "axial", "azim", None),
            P("axial", "azim", None),
            P(),
            P(),
            P("axial", "azim"),
            P("axial", "azim", None, None),
            P("axial", "azim", None, None),
            P("axial", "azim", None, None),
            P("axial", "azim", None, None),
            P(),
            P("axial", "azim", None, None),
            P("axial", "azim", None, None),
        ),
        out_specs=(
            P(None, "axial", "azim", None),
            P(None, "axial", "azim", None),
            P("axial", "azim", None, None),
        ),
        check_vma=False,
    )
```

profile of v0, /device:TPU:6, one launch (start us, length us, event | category | flops | bytes accessed | tf_op | source)
XLA Modules:
  0.0 145.2 jit_solution(12874545248161447015)
XLA Ops:
  0.6 0.0 copy-start
  0.6 1.7 %copy_multiply_fusion.2 = f32[12,4,16,256]{3,0,2,1:T(8,128)S(1)} fusion(f32[12,4,16,256]{3,2,1,0:T(8,128)} %param.13), kind=kLoop, calls=%fused_computation.36 | loop fusion | flops 196608 | bytes 1572864 | tf_op jit(solution)/shard_map/div | solution.py:44
  2.3 0.0 copy-start.10
  2.4 0.0 copy-start.11
  2.4 15.9 %collective-permute-start = (f32[12,1,16,256]{3,0,2,1:T(8,128)S(1)}, f32[12,1,16,256]{3,0,2,1:T(8,128)}, u32[]{:S(2)}, u32[]{:S(2)}) collective-permute-start(f32[12,1,16,256]{3,0,2,1:T(8,128)S(1)} %get-tuple-element.25), channel_id=1, source_target_pairs={{8,0},{16,8},{24,16},{32,24},{40,32},{48,40},{56,48},{64,56},{72,6... | collective-permute-start | bytes 589832 | tf_op jit(solution)/shard_map/ppermute | solution.py:23
  18.3 1.9 %collective-permute-start.1 = (f32[12,1,16,256]{3,0,2,1:T(8,128)S(1)}, f32[12,1,16,256]{3,0,2,1:T(8,128)}, u32[]{:S(2)}, u32[]{:S(2)}) collective-permute-start(f32[12,1,16,256]{3,0,2,1:T(8,128)S(1)} %get-tuple-element.26), channel_id=1, source_target_pairs={{0,8},{8,16},{16,24},{24,32},{32,40},{40,48},{48,56},{56,64},{64,7... | collective-permute-start | bytes 589832 | tf_op jit(solution)/shard_map/ppermute | solution.py:21
  20.2 4.4 %collective-permute-start.2 = (f32[12,4,1,256]{3,0,2,1:T(8,128)S(1)}, f32[12,4,1,256]{3,0,2,1:T(8,128)S(1)}, u32[]{:S(2)}, u32[]{:S(2)}) collective-permute-start(f32[12,4,1,256]{3,0,2,1:T(8,128)S(1)} %get-tuple-element.27), channel_id=1, source_target_pairs={{1,0},{2,1},{3,2},{4,3},{5,4},{6,5},{7,6},{0,7},{9,8},{10,9},{11,1... | collective-permute-start | bytes 147464 | tf_op jit(solution)/shard_map/ppermute | solution.py:23
  24.7 1.9 %collective-permute-start.3 = (f32[12,4,1,256]{3,0,2,1:T(8,128)S(1)}, f32[12,4,1,256]{3,0,2,1:T(8,128)}, u32[]{:S(2)}, u32[]{:S(2)}) collective-permute-start(f32[12,4,1,256]{3,0,2,1:T(8,128)S(1)} %get-tuple-element.28), channel_id=1, source_target_pairs={{0,1},{1,2},{2,3},{3,4},{4,5},{5,6},{6,7},{7,0},{8,9},{9,10},{10,1... | collective-permute-start | bytes 147464 | tf_op jit(solution)/shard_map/ppermute | solution.py:21
  26.6 0.1 copy.80
  26.7 0.1 eq.60
  26.8 0.1 reshape.190
  27.7 1.3 reduce-window.6
  28.9 0.2 slice_reduce_fusion
  29.2 0.1 bitcast_bitcast_fusion
  29.4 0.1 fusion.79
  29.4 0.1 copy.84
  29.5 0.1 reshape.223
  29.7 0.0 copy-start.7
  29.7 0.0 copy-start.12
  29.7 22.3 %scatter_fusion = s32[96,5]{0,1:T(8,128)S(1)} fusion(s32[96,5]{0,1:T(8,128)S(1)} %broadcast_in_dim.41, s32[480]{0:T(512)S(1)} %bitcast.94, s32[480]{0:T(512)S(1)} %reshape.223), kind=kCustom, calls=%fused_computation.3 | custom fusion | bytes 9600 | tf_op jit(solution)/shard_map/scatter | solution.py:103
  52.0 0.0 copy-start.1
  52.0 0.7 copy.85
  52.7 10.3 %all-to-all-start = ((s32[96,1,5]{2,1,0:T(1,128)}), s32[96,1,5]{2,1,0:T(1,128)S(1)}, u32[]{:S(2)}, u32[]{:S(2)}) async-start(s32[96,1,5]{2,1,0:T(1,128)} %copy.85), calls=%async_computation | async-start | bytes 98304 | tf_op jit(solution)/shard_map/all_to_all | solution.py:105
  63.1 0.1 fusion.75
  63.2 0.1 copy.90
  63.3 10.3 %all-to-all-done = s32[96,1,5]{2,1,0:T(1,128)S(1)} async-done(((s32[96,1,5]{2,1,0:T(1,128)}), s32[96,1,5]{2,1,0:T(1,128)S(1)}, u32[]{:S(2)}, u32[]{:S(2)}) %all-to-all-start) | async-done | bytes 1952 | tf_op jit(solution)/shard_map/all_to_all | solution.py:105
  73.6 0.1 copy.86
  73.7 0.1 copy.89
  73.8 0.2 reshape.207
  74.0 0.0 copy-start.2
  74.0 0.0 copy-start.17
  74.0 1.5 %gather_fusion.1 = bf16[480,128]{1,0:T(8,128)(2,1)S(1)} fusion(bf16[120,128]{1,0:T(8,128)(2,1)S(1)} %bitcast.93, s32[1024]{0:T(1024)S(1)} %pad_clamp_fusion.1), kind=kCustom, calls=%fused_computation.1 | custom fusion | bytes 247680 | tf_op jit(solution)/shard_map/gather | solution.py:106
  75.5 0.0 copy-start.15
  75.5 0.1 reshape.206
  75.6 0.1 copy.87
  75.7 0.8 broadcast_select_fusion
  76.5 8.1 %all-to-all-start.1 = ((bf16[96,5,128]{2,1,0:T(8,128)(2,1)}), bf16[96,5,128]{2,1,0:T(8,128)(2,1)S(1)}, u32[]{:S(2)}, u32[]{:S(2)}) async-start(bf16[96,5,128]{2,1,0:T(8,128)(2,1)} %broadcast_select_fusion), calls=%async_computation.1 | async-start | bytes 393216 | tf_op jit(solution)/shard_map/all_to_all | solution.py:108
  84.7 0.0 collective-permute-done.2
  84.7 0.0 collective-permute-done.3
  84.7 7.2 %fusion.52 = (f32[12,4,16,256]{3,0,2,1:T(8,128)S(1)}, f32[12,4,16,256]{3,0,2,1:T(8,128)}) fusion(f32[12,4,16,256]{3,2,1,0:T(8,128)S(1)} %copy-done.2, f32[12,4,16,256]{3,0,2,1:T(8,128)S(1)} %copy_multiply_fusion.2, f32[12,4,1,256]{3,0,2,1:T(8,128)} %collective-permute-done.3, f32[12,4,1,256]{3,0,2,1:T(8,128)S(1)} %collective-permute-done.2, ...), kind=kOutput, calls=%fused_computation.46 | convolution fusion | flops 117768192 | bytes 6038016 | tf_op jit(solution)/shard_map/mfg,mgazr->fazr/dot_general | solution.py:35
  92.0 5.8 %collective-permute-start.4 = (f32[12,1,16,256]{3,0,2,1:T(8,128)S(1)}, f32[12,1,16,256]{3,0,2,1:T(8,128)S(1)}, u32[]{:S(2)}, u32[]{:S(2)}) collective-permute-start(f32[12,1,16,256]{3,0,2,1:T(8,128)S(1)} %get-tuple-element.21), channel_id=1, source_target_pairs={{8,0},{16,8},{24,16},{32,24},{40,32},{48,40},{56,48},{64,56},{72,6... | collective-permute-start | bytes 589832 | tf_op jit(solution)/shard_map/ppermute | solution.py:23
  97.8 1.9 %collective-permute-start.5 = (f32[12,1,16,256]{3,0,2,1:T(8,128)S(1)}, f32[12,1,16,256]{3,0,2,1:T(8,128)}, u32[]{:S(2)}, u32[]{:S(2)}) collective-permute-start(f32[12,1,16,256]{3,0,2,1:T(8,128)S(1)} %get-tuple-element.22), channel_id=1, source_target_pairs={{0,8},{8,16},{16,24},{24,32},{32,40},{40,48},{48,56},{56,64},{64,7... | collective-permute-start | bytes 589832 | tf_op jit(solution)/shard_map/ppermute | solution.py:21
  99.7 3.8 %collective-permute-start.6 = (f32[12,4,1,256]{3,0,2,1:T(8,128)S(1)}, f32[12,4,1,256]{3,0,2,1:T(8,128)S(1)}, u32[]{:S(2)}, u32[]{:S(2)}) collective-permute-start(f32[12,4,1,256]{3,0,2,1:T(8,128)S(1)} %get-tuple-element.23), channel_id=1, source_target_pairs={{1,0},{2,1},{3,2},{4,3},{5,4},{6,5},{7,6},{0,7},{9,8},{10,9},{11,1... | collective-permute-start | bytes 147464 | tf_op jit(solution)/shard_map/ppermute | solution.py:23
  103.5 2.1 %collective-permute-start.7 = (f32[12,4,1,256]{3,0,2,1:T(8,128)S(1)}, f32[12,4,1,256]{3,0,2,1:T(8,128)S(1)}, u32[]{:S(2)}, u32[]{:S(2)}) collective-permute-start(f32[12,4,1,256]{3,0,2,1:T(8,128)S(1)} %get-tuple-element.24), channel_id=1, source_target_pairs={{0,1},{1,2},{2,3},{3,4},{4,5},{5,6},{6,7},{7,0},{8,9},{9,10},{10,1... | collective-permute-start | bytes 147464 | tf_op jit(solution)/shard_map/ppermute | solution.py:21
  105.6 0.1 reshape.194
  105.7 1.5 %gather_fusion.2 = bf16[480,128]{1,0:T(8,128)(2,1)S(1)} fusion(bf16[480,128]{1,0:T(8,128)(2,1)S(1)} %reshape.194, s32[1024]{0:T(1024)S(1)} %pad_clamp_fusion), kind=kCustom, calls=%fused_computation.2 | custom fusion | bytes 247680 | tf_op jit(solution)/shard_map/gather | solution.py:110
  107.2 0.0 copy-start.13
  107.2 0.0 copy-start.16
  107.3 0.0 copy-start.18
  107.3 1.1 convolution_bitcast_fusion
  108.3 3.7 %collective-permute-done.7 = f32[12,4,1,256]{3,0,2,1:T(8,128)S(1)} collective-permute-done((f32[12,4,1,256]{3,0,2,1:T(8,128)S(1)}, f32[12,4,1,256]{3,0,2,1:T(8,128)S(1)}, u32[]{:S(2)}, u32[]{:S(2)}) %collective-permute-start.7) | collective-permute-done | bytes 49184 | tf_op jit(solution)/shard_map/ppermute | solution.py:21
  112.1 7.3 %multiply_add_fusion = (f32[12,4,16,256]{3,0,2,1:T(8,128)S(1)}, f32[12,4,16,256]{3,0,2,1:T(8,128)S(1)}, f32[12,4,16,256]{3,0,2,1:T(8,128)}) fusion(f32[12,4,16,256]{3,0,2,1:T(8,128)S(1)} %copy-done.4, f32[12,4,16,256]{3,2,1,0:T(8,128)S(1)} %copy-done.2, f32[12,4,16,256]{3,0,2,1:T(8,128)} %get-tuple-element.32, ...), kind=kOutput, calls=%fused_computation.80 | convolution fusion | flops 118358016 | bytes 7692800 | tf_op jit(solution)/shard_map/mfg,mgazr->fazr/dot_general | solution.py:35
  119.5 6.0 %collective-permute-start.8 = (f32[12,1,16,256]{3,0,2,1:T(8,128)S(1)}, f32[12,1,16,256]{3,0,2,1:T(8,128)S(1)}, u32[]{:S(2)}, u32[]{:S(2)}) collective-permute-start(f32[12,1,16,256]{3,0,2,1:T(8,128)S(1)} %get-tuple-element.17), channel_id=1, source_target_pairs={{8,0},{16,8},{24,16},{32,24},{40,32},{48,40},{56,48},{64,56},{72,6... | collective-permute-start | bytes 589832 | tf_op jit(solution)/shard_map/ppermute | solution.py:23
  125.5 1.9 %collective-permute-start.9 = (f32[12,1,16,256]{3,0,2,1:T(8,128)S(1)}, f32[12,1,16,256]{3,0,2,1:T(8,128)}, u32[]{:S(2)}, u32[]{:S(2)}) collective-permute-start(f32[12,1,16,256]{3,0,2,1:T(8,128)S(1)} %get-tuple-element.18), channel_id=1, source_target_pairs={{0,8},{8,16},{16,24},{24,32},{32,40},{40,48},{48,56},{56,64},{64,7... | collective-permute-start | bytes 589832 | tf_op jit(solution)/shard_map/ppermute | solution.py:21
  127.4 0.5 slice_reduce_fusion.1
  127.8 0.1 reshape_squeeze.3
  127.9 2.9 %collective-permute-start.10 = (f32[12,4,1,256]{3,0,2,1:T(8,128)S(1)}, f32[12,4,1,256]{3,0,2,1:T(8,128)S(1)}, u32[]{:S(2)}, u32[]{:S(2)}) collective-permute-start(f32[12,4,1,256]{3,0,2,1:T(8,128)S(1)} %get-tuple-element.19), channel_id=1, source_target_pairs={{1,0},{2,1},{3,2},{4,3},{5,4},{6,5},{7,6},{0,7},{9,8},{10,9},{11,1... | collective-permute-start | bytes 147464 | tf_op jit(solution)/shard_map/ppermute | solution.py:23
  130.8 2.1 %collective-permute-start.11 = (f32[12,4,1,256]{3,0,2,1:T(8,128)S(1)}, f32[12,4,1,256]{3,0,2,1:T(8,128)S(1)}, u32[]{:S(2)}, u32[]{:S(2)}) collective-permute-start(f32[12,4,1,256]{3,0,2,1:T(8,128)S(1)} %get-tuple-element.20), channel_id=1, source_target_pairs={{0,1},{1,2},{2,3},{3,4},{4,5},{5,6},{6,7},{7,0},{8,9},{9,10},{10,1... | collective-permute-start | bytes 147464 | tf_op jit(solution)/shard_map/ppermute | solution.py:21
  133.0 1.2 gather_fusion
  134.2 1.0 fusion.51
  135.3 1.3 copy.92
  136.6 1.9 %collective-permute-done.11 = f32[12,4,1,256]{3,0,2,1:T(8,128)S(1)} collective-permute-done((f32[12,4,1,256]{3,0,2,1:T(8,128)S(1)}, f32[12,4,1,256]{3,0,2,1:T(8,128)S(1)}, u32[]{:S(2)}, u32[]{:S(2)}) %collective-permute-start.11) | collective-permute-done | bytes 49184 | tf_op jit(solution)/shard_map/ppermute | solution.py:21
  138.5 5.3 %fusion.45 = f32[12,4,16,256]{3,0,2,1:T(8,128)S(1)} fusion(f32[12,4,16,256]{3,0,2,1:T(8,128)} %get-tuple-element.33, f32[12,4,16,256]{3,0,2,1:T(8,128)S(1)} %copy-done.6, f32[4,4,16,256]{3,0,2,1:T(4,128)S(1)} %fusion.75, f32[12,4,16,256]{3,2,1,0:T(8,128)S(1)} %copy-done.14, f32[12,4,1,256]{3,0,2,1:T(8,128)S(1)} %collective-permute-done.11, ...), kind=kOutput, calls=%fused_computation.33 | convolution fusion | flops 117178368 | bytes 5333504 | tf_op jit(solution)/shard_map/mfg,mgazr->fazr/dot_general | solution.py:35
  143.9 1.3 copy.93
  (56 shorter events, 0.4 us)
Async XLA Ops:
  0.6 133.6 %copy-start = (bf16[8,128,128]{2,1,0:T(8,128)(2,1)S(1)}, bf16[8,128,128]{2,1,0:T(8,128)(2,1)}, u32[]{:S(2)}) copy-start(bf16[8,128,128]{2,1,0:T(8,128)(2,1)} %param.23) | copy-start | bytes 786436
  2.3 24.3 %copy-start.10 = (s32[1,1,120,4]{2,3,1,0:T(4,128)S(1)}, s32[1,1,120,4]{2,3,1,0:T(4,128)}, u32[]{:S(2)}) copy-start(s32[1,1,120,4]{2,3,1,0:T(4,128)} %param.19) | copy-start | bytes 5764
  2.4 27.0 %copy-start.11 = (s32[1,1,120,4]{2,3,1,0:T(4,128)S(1)}, s32[1,1,120,4]{2,3,1,0:T(4,128)}, u32[]{:S(2)}) copy-start(s32[1,1,120,4]{2,3,1,0:T(4,128)} %param.20) | copy-start | bytes 5764
  2.4 82.3 %collective-permute-start = (f32[12,1,16,256]{3,0,2,1:T(8,128)S(1)}, f32[12,1,16,256]{3,0,2,1:T(8,128)}, u32[]{:S(2)}, u32[]{:S(2)}) collective-permute-start(f32[12,1,16,256]{3,0,2,1:T(8,128)S(1)} %get-tuple-element.25), channel_id=1, source_target_pairs={{8,0},{16,8},{24,16},{32,24},{40,32},{48,40},{56,48},{64,56},{72,6... | collective-permute-start | bytes 589832 | tf_op jit(solution)/shard_map/ppermute | solution.py:23
  18.3 66.4 %collective-permute-start.1 = (f32[12,1,16,256]{3,0,2,1:T(8,128)S(1)}, f32[12,1,16,256]{3,0,2,1:T(8,128)}, u32[]{:S(2)}, u32[]{:S(2)}) collective-permute-start(f32[12,1,16,256]{3,0,2,1:T(8,128)S(1)} %get-tuple-element.26), channel_id=1, source_target_pairs={{0,8},{8,16},{16,24},{24,32},{32,40},{40,48},{48,56},{56,64},{64,7... | collective-permute-start | bytes 589832 | tf_op jit(solution)/shard_map/ppermute | solution.py:21
  20.2 64.4 %collective-permute-start.2 = (f32[12,4,1,256]{3,0,2,1:T(8,128)S(1)}, f32[12,4,1,256]{3,0,2,1:T(8,128)S(1)}, u32[]{:S(2)}, u32[]{:S(2)}) collective-permute-start(f32[12,4,1,256]{3,0,2,1:T(8,128)S(1)} %get-tuple-element.27), channel_id=1, source_target_pairs={{1,0},{2,1},{3,2},{4,3},{5,4},{6,5},{7,6},{0,7},{9,8},{10,9},{11,1... | collective-permute-start | bytes 147464 | tf_op jit(solution)/shard_map/ppermute | solution.py:23
  24.7 60.0 %collective-permute-start.3 = (f32[12,4,1,256]{3,0,2,1:T(8,128)S(1)}, f32[12,4,1,256]{3,0,2,1:T(8,128)}, u32[]{:S(2)}, u32[]{:S(2)}) collective-permute-start(f32[12,4,1,256]{3,0,2,1:T(8,128)S(1)} %get-tuple-element.28), channel_id=1, source_target_pairs={{0,1},{1,2},{2,3},{3,4},{4,5},{5,6},{6,7},{7,0},{8,9},{9,10},{10,1... | collective-permute-start | bytes 147464 | tf_op jit(solution)/shard_map/ppermute | solution.py:21
  29.7 33.4 %copy-start.7 = (s32[4,16,256]{2,1,0:T(8,128)S(1)}, s32[4,16,256]{2,1,0:T(8,128)}, u32[]{:S(2)}) copy-start(s32[4,16,256]{2,1,0:T(8,128)} %param.15) | copy-start | bytes 196612
  29.7 33.5 %copy-start.12 = (s32[1,1,120,4]{2,3,1,0:T(4,128)S(1)}, s32[1,1,120,4]{2,3,1,0:T(4,128)}, u32[]{:S(2)}) copy-start(s32[1,1,120,4]{2,3,1,0:T(4,128)} %param.21) | copy-start | bytes 5764
  52.0 21.9 %copy-start.1 = (bf16[1,1,120,128]{3,2,1,0:T(8,128)(2,1)S(1)}, bf16[1,1,120,128]{3,2,1,0:T(8,128)(2,1)}, u32[]{:S(2)}) copy-start(bf16[1,1,120,128]{3,2,1,0:T(8,128)(2,1)} %param.22) | copy-start | bytes 92164
  52.7 20.8 %all-to-all-start = ((s32[96,1,5]{2,1,0:T(1,128)}), s32[96,1,5]{2,1,0:T(1,128)S(1)}, u32[]{:S(2)}, u32[]{:S(2)}) async-start(s32[96,1,5]{2,1,0:T(1,128)} %copy.85), calls=%async_computation | async-start | bytes 98304 | tf_op jit(solution)/shard_map/all_to_all | solution.py:105
  74.0 10.7 %copy-start.2 = (f32[12,4,16,256]{3,2,1,0:T(8,128)S(1)}, f32[12,4,16,256]{3,2,1,0:T(8,128)}, u32[]{:S(2)}) copy-start(f32[12,4,16,256]{3,2,1,0:T(8,128)} %param.13) | copy-start | bytes 2359300
  74.0 10.7 %copy-start.17 = (f32[12]{0:T(128)S(1)}, f32[12]{0:T(128)}, u32[]{:S(2)}) copy-start(f32[12]{0:T(128)} %param.16) | copy-start | bytes 148
  75.5 9.2 %copy-start.15 = (f32[4,12,12]{2,0,1:T(4,128)S(1)}, f32[4,12,12]{2,0,1:T(4,128)}, u32[]{:S(2)}) copy-start(f32[4,12,12]{2,0,1:T(4,128)} %param.17) | copy-start | bytes 6916
  76.5 29.1 %all-to-all-start.1 = ((bf16[96,5,128]{2,1,0:T(8,128)(2,1)}), bf16[96,5,128]{2,1,0:T(8,128)(2,1)S(1)}, u32[]{:S(2)}, u32[]{:S(2)}) async-start(bf16[96,5,128]{2,1,0:T(8,128)(2,1)} %broadcast_select_fusion), calls=%async_computation.1 | async-start | bytes 393216 | tf_op jit(solution)/shard_map/all_to_all | solution.py:108
  91.9 11.6 %copy-start.3 = (f32[12,4,16,256]{3,0,2,1:T(8,128)}, f32[12,4,16,256]{3,0,2,1:T(8,128)S(1)}, u32[]{:S(2)}) copy-start(f32[12,4,16,256]{3,0,2,1:T(8,128)S(1)} %get-tuple-element.31) | copy-start | bytes 2359300
  92.0 20.0 %collective-permute-start.4 = (f32[12,1,16,256]{3,0,2,1:T(8,128)S(1)}, f32[12,1,16,256]{3,0,2,1:T(8,128)S(1)}, u32[]{:S(2)}, u32[]{:S(2)}) collective-permute-start(f32[12,1,16,256]{3,0,2,1:T(8,128)S(1)} %get-tuple-element.21), channel_id=1, source_target_pairs={{8,0},{16,8},{24,16},{32,24},{40,32},{48,40},{56,48},{64,56},{72,6... | collective-permute-start | bytes 589832 | tf_op jit(solution)/shard_map/ppermute | solution.py:23
  97.8 14.3 %collective-permute-start.5 = (f32[12,1,16,256]{3,0,2,1:T(8,128)S(1)}, f32[12,1,16,256]{3,0,2,1:T(8,128)}, u32[]{:S(2)}, u32[]{:S(2)}) collective-permute-start(f32[12,1,16,256]{3,0,2,1:T(8,128)S(1)} %get-tuple-element.22), channel_id=1, source_target_pairs={{0,8},{8,16},{16,24},{24,32},{32,40},{40,48},{48,56},{56,64},{64,7... | collective-permute-start | bytes 589832 | tf_op jit(solution)/shard_map/ppermute | solution.py:21
  99.7 8.6 %collective-permute-start.6 = (f32[12,4,1,256]{3,0,2,1:T(8,128)S(1)}, f32[12,4,1,256]{3,0,2,1:T(8,128)S(1)}, u32[]{:S(2)}, u32[]{:S(2)}) collective-permute-start(f32[12,4,1,256]{3,0,2,1:T(8,128)S(1)} %get-tuple-element.23), channel_id=1, source_target_pairs={{1,0},{2,1},{3,2},{4,3},{5,4},{6,5},{7,6},{0,7},{9,8},{10,9},{11,1... | collective-permute-start | bytes 147464 | tf_op jit(solution)/shard_map/ppermute | solution.py:23
  103.5 8.5 %collective-permute-start.7 = (f32[12,4,1,256]{3,0,2,1:T(8,128)S(1)}, f32[12,4,1,256]{3,0,2,1:T(8,128)S(1)}, u32[]{:S(2)}, u32[]{:S(2)}) collective-permute-start(f32[12,4,1,256]{3,0,2,1:T(8,128)S(1)} %get-tuple-element.24), channel_id=1, source_target_pairs={{0,1},{1,2},{2,3},{3,4},{4,5},{5,6},{6,7},{7,0},{8,9},{9,10},{10,1... | collective-permute-start | bytes 147464 | tf_op jit(solution)/shard_map/ppermute | solution.py:21
  107.2 4.8 %copy-start.4 = (f32[12,4,16,256]{3,0,2,1:T(8,128)S(1)}, f32[12,4,16,256]{3,0,2,1:T(8,128)}, u32[]{:S(2)}) copy-start(f32[12,4,16,256]{3,0,2,1:T(8,128)} %copy-done.3) | copy-start | bytes 2359300
  107.2 4.8 %copy-start.13 = (f32[12,4,16,256]{3,2,1,0:T(8,128)S(1)}, f32[12,4,16,256]{3,2,1,0:T(8,128)}, u32[]{:S(2)}) copy-start(f32[12,4,16,256]{3,2,1,0:T(8,128)} %param.14) | copy-start | bytes 2359300
  107.2 4.8 %copy-start.16 = (f32[4,12,12]{2,0,1:T(4,128)S(1)}, f32[4,12,12]{2,0,1:T(4,128)}, u32[]{:S(2)}) copy-start(f32[4,12,12]{2,0,1:T(4,128)} %param.17) | copy-start | bytes 6916
  107.3 4.8 %copy-start.18 = (f32[12]{0:T(128)S(1)}, f32[12]{0:T(128)}, u32[]{:S(2)}) copy-start(f32[12]{0:T(128)} %param.16) | copy-start | bytes 148
  119.4 8.0 %copy-start.5 = (f32[12,4,16,256]{3,0,2,1:T(8,128)}, f32[12,4,16,256]{3,0,2,1:T(8,128)S(1)}, u32[]{:S(2)}) copy-start(f32[12,4,16,256]{3,0,2,1:T(8,128)S(1)} %get-tuple-element.15) | copy-start | bytes 2359300
  119.4 14.8 %copy-start.8 = (f32[1,1,120,128]{3,2,1,0:T(8,128)S(1)}, f32[1,1,120,128]{3,2,1,0:T(8,128)}, u32[]{:S(2)}) copy-start(f32[1,1,120,128]{3,2,1,0:T(8,128)} %param.25) | copy-start | bytes 184324
  119.4 14.8 %copy-start.9 = (f32[1,1,120,128]{3,2,1,0:T(8,128)S(1)}, f32[1,1,120,128]{3,2,1,0:T(8,128)}, u32[]{:S(2)}) copy-start(f32[1,1,120,128]{3,2,1,0:T(8,128)} %param.24) | copy-start | bytes 184324
  119.5 19.1 %collective-permute-start.8 = (f32[12,1,16,256]{3,0,2,1:T(8,128)S(1)}, f32[12,1,16,256]{3,0,2,1:T(8,128)S(1)}, u32[]{:S(2)}, u32[]{:S(2)}) collective-permute-start(f32[12,1,16,256]{3,0,2,1:T(8,128)S(1)} %get-tuple-element.17), channel_id=1, source_target_pairs={{8,0},{16,8},{24,16},{32,24},{40,32},{48,40},{56,48},{64,56},{72,6... | collective-permute-start | bytes 589832 | tf_op jit(solution)/shard_map/ppermute | solution.py:23
  125.5 13.1 %collective-permute-start.9 = (f32[12,1,16,256]{3,0,2,1:T(8,128)S(1)}, f32[12,1,16,256]{3,0,2,1:T(8,128)}, u32[]{:S(2)}, u32[]{:S(2)}) collective-permute-start(f32[12,1,16,256]{3,0,2,1:T(8,128)S(1)} %get-tuple-element.18), channel_id=1, source_target_pairs={{0,8},{8,16},{16,24},{24,32},{32,40},{40,48},{48,56},{56,64},{64,7... | collective-permute-start | bytes 589832 | tf_op jit(solution)/shard_map/ppermute | solution.py:21
  127.9 8.7 %collective-permute-start.10 = (f32[12,4,1,256]{3,0,2,1:T(8,128)S(1)}, f32[12,4,1,256]{3,0,2,1:T(8,128)S(1)}, u32[]{:S(2)}, u32[]{:S(2)}) collective-permute-start(f32[12,4,1,256]{3,0,2,1:T(8,128)S(1)} %get-tuple-element.19), channel_id=1, source_target_pairs={{1,0},{2,1},{3,2},{4,3},{5,4},{6,5},{7,6},{0,7},{9,8},{10,9},{11,1... | collective-permute-start | bytes 147464 | tf_op jit(solution)/shard_map/ppermute | solution.py:23
  130.8 7.7 %collective-permute-start.11 = (f32[12,4,1,256]{3,0,2,1:T(8,128)S(1)}, f32[12,4,1,256]{3,0,2,1:T(8,128)S(1)}, u32[]{:S(2)}, u32[]{:S(2)}) collective-permute-start(f32[12,4,1,256]{3,0,2,1:T(8,128)S(1)} %get-tuple-element.20), channel_id=1, source_target_pairs={{0,1},{1,2},{2,3},{3,4},{4,5},{5,6},{6,7},{7,0},{8,9},{9,10},{10,1... | collective-permute-start | bytes 147464 | tf_op jit(solution)/shard_map/ppermute | solution.py:21
  135.3 3.2 %copy-start.6 = (f32[12,4,16,256]{3,0,2,1:T(8,128)S(1)}, f32[12,4,16,256]{3,0,2,1:T(8,128)}, u32[]{:S(2)}) copy-start(f32[12,4,16,256]{3,0,2,1:T(8,128)} %copy-done.5) | copy-start | bytes 2359300
  135.3 3.2 %copy-start.14 = (f32[12,4,16,256]{3,2,1,0:T(8,128)S(1)}, f32[12,4,16,256]{3,2,1,0:T(8,128)}, u32[]{:S(2)}) copy-start(f32[12,4,16,256]{3,2,1,0:T(8,128)} %param.14) | copy-start | bytes 2359300
where the time goes:
time: 146 us; the launch traced here: 145 us
  starting transfers between devices  69 us (47%)
  local copies, waits for them, and re-layouts  32.2 us (22%)
  matrix products  22 us (15%)
  waiting for transfers between devices  15.9 us (11%)
  other arithmetic  4.25 us (3%)
  between operations  1.93 us (1%)
    ppermute x6, starting transfers between devices, extended(): lax.ppermute(head, axis, [((i + 1) % count, i) for i in range(ends)])  38.7 us
    scatter x1, local copies, waits for them, and re-layouts, body(): asked = jnp.full((owners_total, cap_slots), -1, jnp.int32).at[target, ran...  22.3 us
    dot_general x3, matrix products, combine(): jnp.einsum('mfg,mgazr->fazr', mixing, weighted, precision=lax.Precision.H...  19.9 us
    ppermute x6, starting transfers between devices, extended(): lax.ppermute(tail, axis, [(i, (i + 1) % count) for i in range(ends)])  11.9 us
    all_to_all x1, starting transfers between devices, body(): lax.all_to_all(asked, 'axial', split_axis=0, concat_axis=0, tiled=True)  10.3 us
    all_to_all x1, waiting for transfers between devices, body(): lax.all_to_all(asked, 'axial', split_axis=0, concat_axis=0, tiled=True)  10.3 us
    all_to_all x1, starting transfers between devices, body(): lax.all_to_all(rows_out, 'axial', split_axis=0, concat_axis=0, tiled=True)  8.1 us
    ppermute x6, waiting for transfers between devices, extended(): lax.ppermute(tail, axis, [(i, (i + 1) % count) for i in range(ends)])  5.57 us
  transfers between devices with their start and end apart: 14, of which 3 were waited for; matrix products, arithmetic and copies ran while one was open for 29% of the time, Pallas kernels for 0%

commit v1 on v0

v1 whole, which is shorter than its diff:
```python
import functools

import jax
import jax.numpy as jnp
from jax import lax
from jax.experimental import pallas as pl
from jax.experimental.pallas import tpu as pltpu
from jax.sharding import PartitionSpec as P

NF = 12
MATS = 4
VIS = 4
NB = 8
ITERS = 3
CA = 4
CZ = 16
CR = 256
PSLOT = 120
RAD = 128
N_AXIAL = 96
N_AZIM = 8
XN = 4
ZN = 12
YN = 2
XY = XN * YN
CAP = 5
ROWS = 8

center_value = 14.2
half_width = 13.8
MESH = pl.DeviceIdType.MESH


def steps():
    spread = center_value / half_width
    ratio = 1.0 / spread
    out = []
    for _ in range(ITERS - 1):
        after = 1.0 / (2.0 * spread - ratio)
        out.append((after * ratio, 2.0 * after / half_width))
        ratio = after
    return out


def kernel(
    source, storage, materials, cond, mixing, counts, owner, slot, block, rad, view,
    emission, reflect,
    x_out, r_out, rad_out,
    dirs, coef, stor, mats, halo_a, halo_z, pack_z,
    ask, ask_a, ask_b, rows_out, rows_a, rows_b, radp, idx, tcol,
    load_sem, sa_send, sa_recv, sz_send, sz_recv,
    qa_send, qa_recv, qb_send, qb_recv, pa_send, pa_recv, pb_send, pb_recv,
):
    ax = lax.axis_index("axial")
    az = lax.axis_index("azim")
    y_pos = ax % YN
    xz = ax // YN
    z_pos = xz % ZN
    x_pos = xz // ZN
    xy_pos = x_pos * YN + y_pos

    def z_peer(k):
        z = (z_pos + k) % ZN
        return z, (x_pos * ZN + z) * YN + y_pos

    def xy_peer(k):
        q = (xy_pos + k) % XY
        return q, ((q // YN) * ZN + z_pos) * YN + q % YN

    before = (ax + N_AXIAL - 1) % N_AXIAL
    after = (ax + 1) % N_AXIAL
    left = (az + N_AZIM - 1) % N_AZIM
    right = (az + 1) % N_AZIM

    loads = [
        pltpu.make_async_copy(source, r_out, load_sem.at[0]),
        pltpu.make_async_copy(materials, mats, load_sem.at[1]),
        pltpu.make_async_copy(storage, stor, load_sem.at[2]),
    ]
    for copy in loads:
        copy.start()

    barrier = pltpu.get_barrier_semaphore()
    for dev in (before, after):
        pl.semaphore_signal(barrier, inc=1, device_id={"axial": dev}, device_id_type=MESH)
    for dev in (left, right):
        pl.semaphore_signal(barrier, inc=1, device_id={"azim": dev}, device_id_type=MESH)
    for k in range(1, ZN):
        pl.semaphore_signal(barrier, inc=1, device_id={"axial": z_peer(k)[1]}, device_id_type=MESH)
    for k in range(1, XY):
        pl.semaphore_signal(barrier, inc=1, device_id={"axial": xy_peer(k)[1]}, device_id_type=MESH)

    def zero_rims(a, carry):
        for it in range(ITERS):
            for f in range(NF):
                dirs[it, f, a, 0:8, :] = jnp.zeros((8, CR), jnp.float32)
                dirs[it, f, a, 24:32, :] = jnp.zeros((8, CR), jnp.float32)
        return carry

    lax.fori_loop(1, CA + 1, zero_rims, 0)
    for it in range(ITERS):
        for f in range(NF):
            dirs[it, f, 0, 8:24, :] = jnp.zeros((CZ, CR), jnp.float32)
            dirs[it, f, CA + 1, 8:24, :] = jnp.zeros((CZ, CR), jnp.float32)

    pl.semaphore_wait(barrier, 4 + (ZN - 1) + (XY - 1))

    def send_axial(it, low, high):
        one = pltpu.make_async_remote_copy(
            low, halo_a.at[it, 1], sa_send.at[it, 0], sa_recv.at[it, 1],
            device_id={"axial": before}, device_id_type=MESH)
        two = pltpu.make_async_remote_copy(
            high, halo_a.at[it, 0], sa_send.at[it, 1], sa_recv.at[it, 0],
            device_id={"axial": after}, device_id_type=MESH)
        one.start()
        two.start()
        return [one, two]

    def send_azim(it):
        one = pltpu.make_async_remote_copy(
            pack_z.at[it, 0], halo_z.at[it, 1], sz_send.at[it, 0], sz_recv.at[it, 1],
            device_id={"azim": left}, device_id_type=MESH)
        two = pltpu.make_async_remote_copy(
            pack_z.at[it, 1], halo_z.at[it, 0], sz_send.at[it, 1], sz_recv.at[it, 0],
            device_id={"azim": right}, device_id_type=MESH)
        one.start()
        two.start()
        return [one, two]

    sent = send_axial(0, source.at[:, 0], source.at[:, CA - 1])
    loads[0].wait()
    for f in range(NF):
        for a in range(CA):
            value = r_out[f, a] * (1.0 / center_value)
            dirs[0, f, a + 1, 8:24, :] = value
            pack_z[0, 0, f, a] = value[0:1, :]
            pack_z[0, 1, f, a] = value[CZ - 1 : CZ, :]
    halos = [sent + send_azim(0)]

    live_count = counts[0, 0]
    lane = lax.broadcasted_iota(jnp.int32, (1, RAD), 1)
    live = lane < live_count
    idx[...] = jnp.zeros((24, RAD), jnp.int32)
    idx[0:VIS, 0:PSLOT] = owner[...]
    idx[8 : 8 + VIS, 0:PSLOT] = slot[...]
    idx[16 : 16 + VIS, 0:PSLOT] = block[...]
    sub96 = lax.broadcasted_iota(jnp.int32, (N_AXIAL, RAD), 0)
    lane96 = lax.broadcasted_iota(jnp.int32, (N_AXIAL, RAD), 1)
    upper = (
        lax.broadcasted_iota(jnp.int32, (RAD, RAD), 0)
        < lax.broadcasted_iota(jnp.int32, (RAD, RAD), 1)
    ).astype(jnp.float32).astype(jnp.bfloat16)
    ones = jnp.ones((RAD, RAD), jnp.bfloat16)
    past = jnp.zeros((N_AXIAL, RAD), jnp.float32)
    hits, ranks = [], []
    tcol[...] = jnp.zeros((RAD, RAD), jnp.float32)
    for k in range(VIS):
        own = idx[k : k + 1, :]
        y_of = own % YN
        t = own // YN
        x_of = (
            (t >= ZN).astype(jnp.int32)
            + (t >= 2 * ZN).astype(jnp.int32)
            + (t >= 3 * ZN).astype(jnp.int32)
        )
        place = (t - ZN * x_of) * XY + x_of * YN + y_of
        place = jnp.where(live, place, -1)
        hit = (sub96 == place).astype(jnp.float32)
        hit_b = hit.astype(jnp.bfloat16)
        rank = jnp.dot(hit_b, upper, preferred_element_type=jnp.float32)
        if k > 0:
            rank = rank + jnp.dot(
                past.astype(jnp.bfloat16), ones, preferred_element_type=jnp.float32)
        past = past + hit
        hits.append(hit)
        ranks.append(rank)
        mine = jnp.sum(hit * rank, axis=0, keepdims=True)
        tcol[k : k + 1, :] = place.astype(jnp.float32) * ROWS + mine
        tcol[8 + k : 9 + k, :] = idx[16 + k : 17 + k, :].astype(jnp.float32)
    asked = jnp.full((N_AXIAL, RAD), -1, jnp.int32)
    for r in range(CAP):
        total = jnp.zeros((N_AXIAL, RAD), jnp.float32)
        for k in range(VIS):
            wanted = (idx[8 + k : 9 + k, :] + 1).astype(jnp.float32)
            total = total + jnp.where(ranks[k] == float(r), hits[k] * wanted, 0.0)
        value = jnp.sum(total, axis=1, keepdims=True).astype(jnp.int32) - 1
        asked = jnp.where(lane96 == r, value, asked)
    ask[...] = asked.reshape(ZN, XY, 1, RAD)
    ask_a[z_pos] = ask[z_pos]
    q_a = []
    for k in range(1, ZN):
        z, dev = z_peer(k)
        copy = pltpu.make_async_remote_copy(
            ask.at[z], ask_a.at[z_pos], qa_send.at[k], qa_recv.at[k],
            device_id={"axial": dev}, device_id_type=MESH)
        copy.start()
        q_a.append(copy)

    for copy in loads[1:]:
        copy.wait()

    def build(a, carry):
        kind = mats[a]
        odd = (kind % 2) == 1
        high = kind >= 2
        for f in range(NF):
            for g in range(NF):
                low_c = jnp.where(odd, mixing[1, f, g], mixing[0, f, g])
                high_c = jnp.where(odd, mixing[3, f, g], mixing[2, f, g])
                value = jnp.where(high, high_c, low_c)
                if f == g:
                    value = value + (stor[f, a] + 6.0 * cond[f])
                coef[f * NF + g, a] = value
        return carry

    lax.fori_loop(0, CA, build, 0)

    lane_c = lax.broadcasted_iota(jnp.int32, (8, CR), 1)
    row_c = lax.broadcasted_iota(jnp.int32, (CZ, CR), 0)

    def interior(it):
        def body(a, carry):
            for h in range(2):
                top = 8 + 8 * h
                held = [dirs[it, g, a + 1, top : top + 8, :] for g in range(NF)]
                for f in range(NF):
                    acc = coef[f * NF, a, 8 * h : 8 * h + 8, :] * held[0]
                    for g in range(1, NF):
                        acc = acc + coef[f * NF + g, a, 8 * h : 8 * h + 8, :] * held[g]
                    near = dirs[it, f, a, top : top + 8, :] + dirs[it, f, a + 2, top : top + 8, :]
                    near = near + dirs[it, f, a + 1, top - 1 : top + 7, :]
                    near = near + dirs[it, f, a + 1, top + 1 : top + 9, :]
                    near = near + jnp.where(lane_c == 0, 0.0, pltpu.roll(held[f], 1, 1))
                    near = near + jnp.where(lane_c == CR - 1, 0.0, pltpu.roll(held[f], CR - 1, 1))
                    r_out[f, a, 8 * h : 8 * h + 8, :] = (
                        r_out[f, a, 8 * h : 8 * h + 8, :] - acc + cond[f] * near)
            return carry

        lax.fori_loop(0, CA, body, 0)

    first = jnp.where(ax == 0, 0.0, 1.0)
    last = jnp.where(ax == N_AXIAL - 1, 0.0, 1.0)
    scalars = steps()

    def finish(it, a):
        gain = 1.0 / center_value if it == 0 else 1.0
        for f in range(NF):
            c = cond[f]
            r = r_out[f, a]
            if a == 0:
                r = r + (c * first * gain) * halo_a[it, 0, f]
            if a == CA - 1:
                r = r + (c * last * gain) * halo_a[it, 1, f]
            r = r + c * (
                jnp.where(row_c == 0, halo_z[it, 0, f, a], 0.0)
                + jnp.where(row_c == CZ - 1, halo_z[it, 1, f, a], 0.0))
            r_out[f, a] = r
            if it + 1 < ITERS:
                alpha, beta = scalars[it]
                old = dirs[it, f, a + 1, 8:24, :]
                new = alpha * old + beta * r
                dirs[it + 1, f, a + 1, 8:24, :] = new
                pack_z[it + 1, 0, f, a] = new[0:1, :]
                pack_z[it + 1, 1, f, a] = new[CZ - 1 : CZ, :]
                if it == ITERS - 2:
                    x_out[f, a] = dirs[0, f, a + 1, 8:24, :] + old + new

    def wait_halos(it):
        for copy in halos[it]:
            copy.wait_recv()

    def advance(it):
        finish(it, 0)
        finish(it, CA - 1)
        nxt = send_axial(
            it + 1, dirs.at[it + 1, :, 1, 8:24, :], dirs.at[it + 1, :, CA, 8:24, :])
        finish(it, 1)
        finish(it, 2)
        halos.append(nxt + send_azim(it + 1))

    interior(0)
    wait_halos(0)
    advance(0)

    for copy in q_a:
        copy.wait_recv()
    ask_b[xy_pos] = ask_a[:, xy_pos]
    q_b = []
    for k in range(1, XY):
        q, dev = xy_peer(k)
        copy = pltpu.make_async_remote_copy(
            ask_a.at[:, q], ask_b.at[xy_pos], qb_send.at[k], qb_recv.at[k],
            device_id={"axial": dev}, device_id_type=MESH)
        copy.start()
        q_b.append(copy)

    radp[...] = jnp.zeros((RAD, RAD), jnp.float32)
    radp[0:PSLOT, :] = rad[...].astype(jnp.float32)
    interior(1)
    for copy in q_b:
        copy.wait_recv()

    panels = radp[...].astype(jnp.bfloat16)
    lane_r = lax.broadcasted_iota(jnp.int32, (ZN, ROWS, RAD), 2)
    sub_r = lax.broadcasted_iota(jnp.int32, (ZN, ROWS, RAD), 1)
    for q in range(XY):
        wanted = jnp.broadcast_to(ask_b[q], (ZN, ROWS, RAD))
        column = jnp.sum(
            jnp.where(lane_r == sub_r, wanted, 0), axis=2, keepdims=True)
        hot = ((lane_r == column) & (sub_r < CAP)).astype(jnp.float32)
        got = jnp.dot(
            hot.reshape(ZN * ROWS, RAD).astype(jnp.bfloat16), panels,
            preferred_element_type=jnp.float32)
        rows_out[q] = got.reshape(ZN, ROWS, RAD).astype(jnp.bfloat16)
    rows_a[xy_pos] = rows_out[xy_pos]
    p_a = []
    for k in range(1, XY):
        q, dev = xy_peer(k)
        copy = pltpu.make_async_remote_copy(
            rows_out.at[q], rows_a.at[xy_pos], pa_send.at[k], pa_recv.at[k],
            device_id={"axial": dev}, device_id_type=MESH)
        copy.start()
        p_a.append(copy)

    wait_halos(1)
    advance(1)

    for copy in p_a:
        copy.wait_recv()
    rows_b[z_pos] = rows_a[:, z_pos]
    p_b = []
    for k in range(1, ZN):
        z, dev = z_peer(k)
        copy = pltpu.make_async_remote_copy(
            rows_a.at[:, z], rows_b.at[z_pos], pb_send.at[k], pb_recv.at[k],
            device_id={"axial": dev}, device_id_type=MESH)
        copy.start()
        p_b.append(copy)

    interior(2)
    wait_halos(2)
    for a in range(CA):
        finish(2, a)

    for copy in p_b:
        copy.wait_recv()
    table = rows_b[...].astype(jnp.float32).reshape(N_AXIAL * ROWS, RAD).astype(jnp.bfloat16)
    columns = jnp.transpose(tcol[...])
    lane_t = lax.broadcasted_iota(jnp.int32, (RAD, N_AXIAL * ROWS), 1).astype(jnp.float32)
    picked, kinds = [], []
    for k in range(VIS):
        pick = (lane_t == columns[:, k : k + 1]).astype(jnp.float32).astype(jnp.bfloat16)
        picked.append(jnp.dot(pick, table, preferred_element_type=jnp.float32))
        kinds.append(columns[:, 8 + k : 9 + k])
    incoming = jnp.zeros((RAD, RAD), jnp.float32)
    for b in range(NB):
        grouped = jnp.zeros((RAD, RAD), jnp.float32)
        for k in range(VIS):
            grouped = grouped + jnp.where(kinds[k] == float(b), picked[k], 0.0)
        major = grouped.astype(jnp.bfloat16)
        minor = (grouped - major.astype(jnp.float32)).astype(jnp.bfloat16)
        for part in (major, minor):
            incoming = incoming + lax.dot_general(
                part, view[b], (((1,), (1,)), ((), ())),
                preferred_element_type=jnp.float32)
    wall = x_out[0, :, :, CR - RAD :].reshape(CA * CZ, RAD)[:, RAD - 1 :]
    wall = jnp.concatenate([wall, wall], axis=0)
    slots = lax.broadcasted_iota(jnp.int32, (PSLOT, RAD), 0)
    result = emission[...] * wall[0:PSLOT] + reflect[...] * incoming[0:PSLOT]
    rad_out[...] = jnp.where(slots < live_count, result, 0.0)

    for group in halos + [q_a, q_b, p_a, p_b]:
        for copy in group:
            copy.wait_send()


def body(
    source, storage, materials, conductance, mixing, counts, vis_owner, vis_slot, vis_block,
    radiosity_old, view_blocks, emission, reflect,
):
    vm = pl.BlockSpec(memory_space=pltpu.VMEM)
    sm = pl.BlockSpec(memory_space=pltpu.SMEM)
    anywhere = pl.BlockSpec(memory_space=pl.ANY)
    dma = pltpu.SemaphoreType.DMA
    f32, i32, b16 = jnp.float32, jnp.int32, jnp.bfloat16
    x, r, rad = pl.pallas_call(
        kernel,
        out_shape=(
            jax.ShapeDtypeStruct((NF, CA, CZ, CR), f32),
            jax.ShapeDtypeStruct((NF, CA, CZ, CR), f32),
            jax.ShapeDtypeStruct((PSLOT, RAD), f32),
        ),
        in_specs=[anywhere, anywhere, anywhere, sm, sm, sm, vm, vm, vm, vm, vm, vm, vm],
        out_specs=(vm, vm, vm),
        scratch_shapes=[
            pltpu.VMEM((ITERS, NF, CA + 2, CZ + 16, CR), f32),
            pltpu.VMEM((NF * NF, CA, CZ, CR), f32),
            pltpu.VMEM((NF, CA, CZ, CR), f32),
            pltpu.VMEM((CA, CZ, CR), i32),
            pltpu.VMEM((ITERS, 2, NF, CZ, CR), f32),
            pltpu.VMEM((ITERS, 2, NF, CA, 1, CR), f32),
            pltpu.VMEM((ITERS, 2, NF, CA, 1, CR), f32),
            pltpu.VMEM((ZN, XY, 1, RAD), i32),
            pltpu.VMEM((ZN, XY, 1, RAD), i32),
            pltpu.VMEM((XY, ZN, 1, RAD), i32),
            pltpu.VMEM((XY, ZN, ROWS, RAD), b16),
            pltpu.VMEM((XY, ZN, ROWS, RAD), b16),
            pltpu.VMEM((ZN, XY, ROWS, RAD), b16),
            pltpu.VMEM((RAD, RAD), f32),
            pltpu.VMEM((24, RAD), i32),
            pltpu.VMEM((RAD, RAD), f32),
            dma((3,)),
            dma((ITERS, 2)), dma((ITERS, 2)), dma((ITERS, 2)), dma((ITERS, 2)),
            dma((ZN,)), dma((ZN,)), dma((XY,)), dma((XY,)),
            dma((XY,)), dma((XY,)), dma((ZN,)), dma((ZN,)),
        ],
        compiler_params=pltpu.CompilerParams(
            collective_id=0, has_side_effects=True, vmem_limit_bytes=56 * 1024 * 1024),
    )(
        source, storage, materials, conductance, mixing, counts,
        vis_owner[0, 0].T, vis_slot[0, 0].T, vis_block[0, 0].T,
        radiosity_old[0, 0], view_blocks, emission[0, 0], reflect[0, 0],
    )
    return x, r, rad[None, None]


def solution(mesh):
    return jax.shard_map(
        body,
        mesh=mesh,
        in_specs=(
            P(None, "axial", "azim", None),
            P(None, "axial", "azim", None),
            P("axial", "azim", None),
            P(),
            P(),
            P("axial", "azim"),
            P("axial", "azim", None, None),
            P("axial", "azim", None, None),
            P("axial", "azim", None, None),
            P("axial", "azim", None, None),
            P(),
            P("axial", "azim", None, None),
            P("axial", "azim", None, None),
        ),
        out_specs=(
            P(None, "axial", "azim", None),
            P(None, "axial", "azim", None),
            P("axial", "azim", None, None),
        ),
        check_vma=False,
    )
```

time: 146 us -> 71 us (0.49)
  the two profiles are of different devices: /device:TPU:6 before, /device:TPU:8 now
where the time goes in v1:
time: 71 us; the launch traced here: 70.7 us
  Pallas kernels  64.4 us (91%)
  local copies, waits for them, and re-layouts  5 us (7%)
  between operations  1.3 us (2%)
    pallas_call x1, Pallas kernels, body(): pl.pallas_call(kernel, out_shape=(jax.ShapeDtypeStruct((NF, CA, CZ, CR),...  64.4 us
    unnamed x8, local copies, waits for them, and re-layouts  5 us

profile of v1, /device:TPU:8, one launch (start us, length us, event | category | flops | bytes accessed | tf_op | source)
XLA Modules:
  0.0 70.7 jit_solution(12141373824746303750)
XLA Ops:
  1.3 1.4 %copy.16.mixing = f32[4,12,12]{2,1,0:T(8,128)} copy(f32[4,12,12]{2,0,1:T(4,128)} %param.17) | data formatting | bytes 4608 | tf_op args[4]
  2.6 64.4 %shard_map.148 = (f32[12,4,16,256]{3,2,1,0:T(8,128)}, f32[12,4,16,256]{3,2,1,0:T(8,128)}, f32[120,128]{1,0:T(8,128)}) custom-call(f32[12,4,16,256]{3,2,1,0:T(8,128)} %source.1, f32[12,4,16,256]{3,2,1,0:T(8,128)} %storage.1, s32[4,16,256]{2,1,0:T(8,128)} %materials.1, f32[12]{0:T(128)} %cond.1, f32[4,12,12]{2,1,0:T(8,128)} %copy.16.mixing, ...), custom_call_target="tpu_custom_call" | custom-call | tf_op jit(solution)/shard_map/pallas_call | solution.py:386
  67.1 0.0 copy-start
  67.1 2.1 %copy.21 = f32[12,4,16,256]{3,2,1,0:T(8,128)} copy(f32[12,4,16,256]{3,2,1,0:T(8,128)} %get-tuple-element.12) | data formatting | bytes 1572864
  69.2 0.0 copy-done
  69.2 0.0 copy-start.1
  69.2 0.9 %copy.22 = f32[12,4,16,256]{3,2,1,0:T(8,128)} copy(f32[12,4,16,256]{3,2,1,0:T(8,128)S(1)} %copy-done) | data formatting | bytes 1572864
  70.1 0.0 copy-done.1
  70.1 0.6 copy.23
Async XLA Ops:
  67.1 2.1 %copy-start = (f32[12,4,16,256]{3,2,1,0:T(8,128)S(1)}, f32[12,4,16,256]{3,2,1,0:T(8,128)}, u32[]{:S(2)}) copy-start(f32[12,4,16,256]{3,2,1,0:T(8,128)} %get-tuple-element.13) | copy-start | bytes 2359300
  69.2 0.9 %copy-start.1 = (f32[120,128]{1,0:T(8,128)S(1)}, f32[120,128]{1,0:T(8,128)}, u32[]{:S(2)}) copy-start(f32[120,128]{1,0:T(8,128)} %get-tuple-element.8) | copy-start | bytes 184324

commit v2 on v1

--- a/solution.py
+++ b/solution.py
@@ -25,6 +25,10 @@
 XY = XN * YN
 CAP = 5
 ROWS = 8
+NCH = 3
+FC = NF // NCH
+BOUND = 24.0
+LEVELS = 32760.0
 
 center_value = 14.2
 half_width = 13.8
@@ -46,9 +50,10 @@
     source, storage, materials, cond, mixing, counts, owner, slot, block, rad, view,
     emission, reflect,
     x_out, r_out, rad_out,
-    dirs, coef, stor, mats, halo_a, halo_z, pack_z,
+    dirs, coef, stor, mats, face_in, face_out, side_in, side_out,
+    fscale_in, fscale_out, sscale_in, sscale_out, side_f, pack_f,
     ask, ask_a, ask_b, rows_out, rows_a, rows_b, radp, idx, tcol,
-    load_sem, sa_send, sa_recv, sz_send, sz_recv,
+    load_sem, fa_send, fa_recv, fs_send, fs_recv, sa_send, sa_recv, ss_send, ss_recv,
     qa_send, qa_recv, qb_send, qb_recv, pa_send, pa_recv, pb_send, pb_recv,
 ):
     ax = lax.axis_index("axial")
@@ -105,37 +110,59 @@
 
     pl.semaphore_wait(barrier, 4 + (ZN - 1) + (XY - 1))
 
-    def send_axial(it, low, high):
-        one = pltpu.make_async_remote_copy(
-            low, halo_a.at[it, 1], sa_send.at[it, 0], sa_recv.at[it, 1],
-            device_id={"axial": before}, device_id_type=MESH)
-        two = pltpu.make_async_remote_copy(
-            high, halo_a.at[it, 0], sa_send.at[it, 1], sa_recv.at[it, 0],
-            device_id={"axial": after}, device_id_type=MESH)
-        one.start()
-        two.start()
-        return [one, two]
-
-    def send_azim(it):
-        one = pltpu.make_async_remote_copy(
-            pack_z.at[it, 0], halo_z.at[it, 1], sz_send.at[it, 0], sz_recv.at[it, 1],
-            device_id={"azim": left}, device_id_type=MESH)
-        two = pltpu.make_async_remote_copy(
-            pack_z.at[it, 1], halo_z.at[it, 0], sz_send.at[it, 1], sz_recv.at[it, 0],
-            device_id={"azim": right}, device_id_type=MESH)
-        one.start()
-        two.start()
-        return [one, two]
-
-    sent = send_axial(0, source.at[:, 0], source.at[:, CA - 1])
+    def fixed(values, inverse):
+        return jnp.round(values * inverse).astype(jnp.int32).astype(jnp.int16)
+
+    def wide(coded):
+        return coded.astype(jnp.int32).astype(jnp.float32)
+
+    halos = {}
+
+    def send_pair(it, c, key, out, into, send, recv, axis, low, high):
+        pair = []
+        for side, dev in ((0, low), (1, high)):
+            copy = pltpu.make_async_remote_copy(
+                out(side), into(1 - side), send.at[it, c, side], recv.at[it, c, 1 - side],
+                device_id={axis: dev}, device_id_type=MESH)
+            copy.start()
+            pair.append(copy)
+        halos[key, it, c] = pair
+
+    def send_sides(it, c):
+        if it > 0:
+            send_pair(
+                it, c, "ss", lambda s: sscale_out.at[it, s, c], lambda s: sscale_in.at[it, s, c],
+                ss_send, ss_recv, "azim", left, right)
+        send_pair(
+            it, c, "sa", lambda s: side_out.at[it, s, c], lambda s: side_in.at[it, s, c],
+            sa_send, sa_recv, "azim", left, right)
+
+    def send_faces(it, c):
+        group = pl.ds(c * FC, FC)
+        if it > 0:
+            send_pair(
+                it, c, "fs", lambda s: fscale_out.at[it, s, c], lambda s: fscale_in.at[it, s, c],
+                fs_send, fs_recv, "axial", before, after)
+        send_pair(
+            it, c, "fa", lambda s: face_out.at[it, s, group], lambda s: face_in.at[it, s, group],
+            fa_send, fa_recv, "axial", before, after)
+
     loads[0].wait()
-    for f in range(NF):
-        for a in range(CA):
-            value = r_out[f, a] * (1.0 / center_value)
-            dirs[0, f, a + 1, 8:24, :] = value
-            pack_z[0, 0, f, a] = value[0:1, :]
-            pack_z[0, 1, f, a] = value[CZ - 1 : CZ, :]
-    halos = [sent + send_azim(0)]
+    for c in range(NCH):
+        for fl in range(FC):
+            f = c * FC + fl
+            for a in range(CA):
+                value = r_out[f, a]
+                dirs[0, f, a + 1, 8:24, :] = value * (1.0 / center_value)
+                row = fl * CA + a
+                pack_f[0, row : row + 1, :] = value[0:1, :]
+                pack_f[1, row : row + 1, :] = value[CZ - 1 : CZ, :]
+                if a in (0, CA - 1):
+                    face_out[0, a // (CA - 1), f] = fixed(value, LEVELS / BOUND)
+        for side in range(2):
+            side_out[0, side, c] = fixed(pack_f[side], LEVELS / BOUND)
+        send_sides(0, c)
+        send_faces(0, c)
 
     live_count = counts[0, 0]
     lane = lax.broadcasted_iota(jnp.int32, (1, RAD), 1)
@@ -205,8 +232,8 @@
         high = kind >= 2
         for f in range(NF):
             for g in range(NF):
-                low_c = jnp.where(odd, mixing[1, f, g], mixing[0, f, g])
-                high_c = jnp.where(odd, mixing[3, f, g], mixing[2, f, g])
+                low_c = jnp.where(odd, mixing[f, 1, g], mixing[f, 0, g])
+                high_c = jnp.where(odd, mixing[f, 3, g], mixing[f, 2, g])
                 value = jnp.where(high, high_c, low_c)
                 if f == g:
                     value = value + (stor[f, a] + 6.0 * cond[f])
@@ -242,46 +269,69 @@
     last = jnp.where(ax == N_AXIAL - 1, 0.0, 1.0)
     scalars = steps()
 
-    def finish(it, a):
-        gain = 1.0 / center_value if it == 0 else 1.0
-        for f in range(NF):
-            c = cond[f]
-            r = r_out[f, a]
-            if a == 0:
-                r = r + (c * first * gain) * halo_a[it, 0, f]
-            if a == CA - 1:
-                r = r + (c * last * gain) * halo_a[it, 1, f]
-            r = r + c * (
-                jnp.where(row_c == 0, halo_z[it, 0, f, a], 0.0)
-                + jnp.where(row_c == CZ - 1, halo_z[it, 1, f, a], 0.0))
-            r_out[f, a] = r
-            if it + 1 < ITERS:
-                alpha, beta = scalars[it]
-                old = dirs[it, f, a + 1, 8:24, :]
-                new = alpha * old + beta * r
-                dirs[it + 1, f, a + 1, 8:24, :] = new
-                pack_z[it + 1, 0, f, a] = new[0:1, :]
-                pack_z[it + 1, 1, f, a] = new[CZ - 1 : CZ, :]
-                if it == ITERS - 2:
-                    x_out[f, a] = dirs[0, f, a + 1, 8:24, :] + old + new
-
-    def wait_halos(it):
-        for copy in halos[it]:
-            copy.wait_recv()
-
-    def advance(it):
-        finish(it, 0)
-        finish(it, CA - 1)
-        nxt = send_axial(
-            it + 1, dirs.at[it + 1, :, 1, 8:24, :], dirs.at[it + 1, :, CA, 8:24, :])
-        finish(it, 1)
-        finish(it, 2)
-        halos.append(nxt + send_azim(it + 1))
-
-    interior(0)
-    wait_halos(0)
-    advance(0)
-
+    unit = BOUND / LEVELS / center_value
+
+    def arrived(key, it, c, side):
+        halos[key, it, c][1 - side].wait_recv()
+
+    def finish(it, c):
+        for side in range(2):
+            if it > 0:
+                arrived("ss", it, c, side)
+            arrived("sa", it, c, side)
+            scale = sscale_in[it, side, c] if it > 0 else unit
+            side_f[side] = wide(side_in[it, side, c]) * scale
+        tops = {}
+        for a in (1, 2, 0, 3):
+            end = a // (CA - 1)
+            if a in (0, CA - 1):
+                if it > 0:
+                    arrived("fs", it, c, end)
+                arrived("fa", it, c, end)
+                scale = fscale_in[it, end, c] if it > 0 else unit
+                scale = scale * (first if a == 0 else last)
+            top = jnp.zeros((CZ, CR), jnp.float32)
+            for fl in range(FC):
+                f = c * FC + fl
+                row = fl * CA + a
+                add = (
+                    jnp.where(row_c == 0, side_f[0, row : row + 1, :], 0.0)
+                    + jnp.where(row_c == CZ - 1, side_f[1, row : row + 1, :], 0.0))
+                if a in (0, CA - 1):
+                    add = add + wide(face_in[it, end, f]) * scale
+                r = r_out[f, a] + cond[f] * add
+                r_out[f, a] = r
+                if it + 1 < ITERS:
+                    alpha, beta = scalars[it]
+                    old = dirs[it, f, a + 1, 8:24, :]
+                    new = alpha * old + beta * r
+                    dirs[it + 1, f, a + 1, 8:24, :] = new
+                    pack_f[0, row : row + 1, :] = new[0:1, :]
+                    pack_f[1, row : row + 1, :] = new[CZ - 1 : CZ, :]
+                    if a in (0, CA - 1):
+                        top = jnp.maximum(top, jnp.abs(new))
+                    if it == ITERS - 2:
+                        x_out[f, a] = dirs[0, f, a + 1, 8:24, :] + old + new
+            tops[a] = top
+        if it + 1 == ITERS:
+            return
+        for side in range(2):
+            rows = pack_f[side]
+            high = jnp.maximum(jnp.max(jnp.abs(rows), axis=0, keepdims=True), 1e-30)
+            sscale_out[it + 1, side, c] = high * (1.0 / LEVELS)
+            side_out[it + 1, side, c] = fixed(rows, LEVELS / high)
+        send_sides(it + 1, c)
+        for end in range(2):
+            a = end * (CA - 1)
+            high = jnp.maximum(jnp.max(tops[a], axis=0, keepdims=True), 1e-30)
+            fscale_out[it + 1, end, c] = high * (1.0 / LEVELS)
+            inverse = LEVELS / high
+            for f in range(c * FC, c * FC + FC):
+                face_out[it + 1, end, f] = fixed(dirs[it + 1, f, a + 1, 8:24, :], inverse)
+        send_faces(it + 1, c)
+
+    radp[...] = jnp.zeros((RAD, RAD), jnp.float32)
+    radp[0:PSLOT, :] = rad[...].astype(jnp.float32)
     for copy in q_a:
         copy.wait_recv()
     ask_b[xy_pos] = ask_a[:, xy_pos]
@@ -294,9 +344,7 @@
         copy.start()
         q_b.append(copy)
 
-    radp[...] = jnp.zeros((RAD, RAD), jnp.float32)
-    radp[0:PSLOT, :] = rad[...].astype(jnp.float32)
-    interior(1)
+    interior(0)
     for copy in q_b:
         copy.wait_recv()
 
@@ -322,8 +370,9 @@
         copy.start()
         p_a.append(copy)
 
-    wait_halos(1)
-    advance(1)
+    for c in range(NCH):
+        finish(0, c)
+    interior(1)
 
     for copy in p_a:
         copy.wait_recv()
@@ -337,10 +386,9 @@
         copy.start()
         p_b.append(copy)
 
+    for c in range(NCH):
+        finish(1, c)
     interior(2)
-    wait_halos(2)
-    for a in range(CA):
-        finish(2, a)
 
     for copy in p_b:
         copy.wait_recv()
@@ -369,7 +417,10 @@
     result = emission[...] * wall[0:PSLOT] + reflect[...] * incoming[0:PSLOT]
     rad_out[...] = jnp.where(slots < live_count, result, 0.0)
 
-    for group in halos + [q_a, q_b, p_a, p_b]:
+    for c in range(NCH):
+        finish(2, c)
+
+    for group in list(halos.values()) + [q_a, q_b, p_a, p_b]:
         for copy in group:
             copy.wait_send()
 
@@ -382,13 +433,13 @@
     sm = pl.BlockSpec(memory_space=pltpu.SMEM)
     anywhere = pl.BlockSpec(memory_space=pl.ANY)
     dma = pltpu.SemaphoreType.DMA
-    f32, i32, b16 = jnp.float32, jnp.int32, jnp.bfloat16
+    f32, i32, i16, b16 = jnp.float32, jnp.int32, jnp.int16, jnp.bfloat16
     x, r, rad = pl.pallas_call(
         kernel,
         out_shape=(
-            jax.ShapeDtypeStruct((NF, CA, CZ, CR), f32),
-            jax.ShapeDtypeStruct((NF, CA, CZ, CR), f32),
-            jax.ShapeDtypeStruct((PSLOT, RAD), f32),
+            pltpu.VMEM((NF, CA, CZ, CR), f32),
+            pltpu.VMEM((NF, CA, CZ, CR), f32),
+            pltpu.VMEM((PSLOT, RAD), f32),
         ),
         in_specs=[anywhere, anywhere, anywhere, sm, sm, sm, vm, vm, vm, vm, vm, vm, vm],
         out_specs=(vm, vm, vm),
@@ -397,9 +448,16 @@
             pltpu.VMEM((NF * NF, CA, CZ, CR), f32),
             pltpu.VMEM((NF, CA, CZ, CR), f32),
             pltpu.VMEM((CA, CZ, CR), i32),
-            pltpu.VMEM((ITERS, 2, NF, CZ, CR), f32),
-            pltpu.VMEM((ITERS, 2, NF, CA, 1, CR), f32),
-            pltpu.VMEM((ITERS, 2, NF, CA, 1, CR), f32),
+            pltpu.VMEM((ITERS, 2, NF, CZ, CR), i16),
+            pltpu.VMEM((ITERS, 2, NF, CZ, CR), i16),
+            pltpu.VMEM((ITERS, 2, NCH, FC * CA, CR), i16),
+            pltpu.VMEM((ITERS, 2, NCH, FC * CA, CR), i16),
+            pltpu.VMEM((ITERS, 2, NCH, 1, CR), f32),
+            pltpu.VMEM((ITERS, 2, NCH, 1, CR), f32),
+            pltpu.VMEM((ITERS, 2, NCH, 1, CR), f32),
+            pltpu.VMEM((ITERS, 2, NCH, 1, CR), f32),
+            pltpu.VMEM((2, FC * CA, CR), f32),
+            pltpu.VMEM((2, FC * CA, CR), f32),
             pltpu.VMEM((ZN, XY, 1, RAD), i32),
             pltpu.VMEM((ZN, XY, 1, RAD), i32),
             pltpu.VMEM((XY, ZN, 1, RAD), i32),
@@ -410,14 +468,14 @@
             pltpu.VMEM((24, RAD), i32),
             pltpu.VMEM((RAD, RAD), f32),
             dma((3,)),
-            dma((ITERS, 2)), dma((ITERS, 2)), dma((ITERS, 2)), dma((ITERS, 2)),
+            *[dma((ITERS, NCH, 2)) for _ in range(8)],
             dma((ZN,)), dma((ZN,)), dma((XY,)), dma((XY,)),
             dma((XY,)), dma((XY,)), dma((ZN,)), dma((ZN,)),
         ],
         compiler_params=pltpu.CompilerParams(
             collective_id=0, has_side_effects=True, vmem_limit_bytes=56 * 1024 * 1024),
     )(
-        source, storage, materials, conductance, mixing, counts,
+        source, storage, materials, conductance, jnp.transpose(mixing, (1, 0, 2)), counts,
         vis_owner[0, 0].T, vis_slot[0, 0].T, vis_block[0, 0].T,
         radiosity_old[0, 0], view_blocks, emission[0, 0], reflect[0, 0],
     )

time: 71 us -> 53.1 us (0.75)
  the two profiles are of different devices: /device:TPU:8 before, /device:TPU:24 now
where the time goes in v2:
time: 53.1 us; the launch traced here: 53 us
  Pallas kernels  49.3 us (93%)
  local copies, waits for them, and re-layouts  2.38 us (4%)
  between operations  1.29 us (2%)
    pallas_call x1, Pallas kernels, body(): pl.pallas_call(kernel, out_shape=(pltpu.VMEM((NF, CA, CZ, CR), f32), pltp...  49.3 us
    unnamed x3, local copies, waits for them, and re-layouts  2.38 us

profile of v2, /device:TPU:24, one launch (start us, length us, event | category | flops | bytes accessed | tf_op | source)
XLA Modules:
  0.0 53.0 jit_solution(9205813158305033052)
XLA Ops:
  1.3 49.3 %shard_map.148 = (f32[12,4,16,256]{3,2,1,0:T(8,128)S(1)}, f32[12,4,16,256]{3,2,1,0:T(8,128)S(1)}, f32[120,128]{1,0:T(8,128)S(1)}) custom-call(f32[12,4,16,256]{3,2,1,0:T(8,128)} %source.1, f32[12,4,16,256]{3,2,1,0:T(8,128)} %storage.1, s32[4,16,256]{2,1,0:T(8,128)} %materials.1, f32[12]{0:T(128)} %cond.1, f32[12,4,12]{2,1,0:T(4,128)} %bitcast.18, ...), custom_call_target="tpu_custom_call" | custom-call | tf_op jit(solution)/shard_map/pallas_call | solution.py:437
  50.6 0.9 %copy.19 = f32[12,4,16,256]{3,2,1,0:T(8,128)} copy(f32[12,4,16,256]{3,2,1,0:T(8,128)S(1)} %get-tuple-element.9) | data formatting | bytes 1572864
  51.5 0.6 %copy.21 = f32[1,1,120,128]{3,2,1,0:T(8,128)} copy(f32[1,1,120,128]{3,2,1,0:T(8,128)S(1)} %bitcast.14) | data formatting | bytes 122880
  52.1 0.9 %copy.20 = f32[12,4,16,256]{3,2,1,0:T(8,128)} copy(f32[12,4,16,256]{3,2,1,0:T(8,128)S(1)} %get-tuple-element.10) | data formatting | bytes 1572864

commit v3 on v2

--- a/solution.py
+++ b/solution.py
@@ -47,12 +47,13 @@
 
 
 def kernel(
-    source, storage, materials, cond, mixing, counts, owner, slot, block, rad, view,
-    emission, reflect,
+    source, storage, materials, cond, mixing, counts, owner_h, slot_h, block_h, rad_h, view_h,
+    emission_h, reflect_h,
     x_out, r_out, rad_out,
     dirs, coef, stor, mats, face_in, face_out, side_in, side_out,
     fscale_in, fscale_out, sscale_in, sscale_out, side_f, pack_f,
     ask, ask_a, ask_b, rows_out, rows_a, rows_b, radp, idx, tcol,
+    owner, slot, block, rad, view, emission, reflect, ask_t,
     load_sem, fa_send, fa_recv, fs_send, fs_recv, sa_send, sa_recv, ss_send, ss_recv,
     qa_send, qa_recv, qb_send, qb_recv, pa_send, pa_recv, pb_send, pb_recv,
 ):
@@ -82,7 +83,18 @@
         pltpu.make_async_copy(materials, mats, load_sem.at[1]),
         pltpu.make_async_copy(storage, stor, load_sem.at[2]),
     ]
-    for copy in loads:
+    index_loads = [
+        pltpu.make_async_copy(owner_h, owner, load_sem.at[3]),
+        pltpu.make_async_copy(slot_h, slot, load_sem.at[4]),
+        pltpu.make_async_copy(block_h, block, load_sem.at[5]),
+    ]
+    panel_loads = [
+        pltpu.make_async_copy(rad_h, rad, load_sem.at[6]),
+        pltpu.make_async_copy(view_h, view, load_sem.at[7]),
+        pltpu.make_async_copy(emission_h, emission, load_sem.at[8]),
+        pltpu.make_async_copy(reflect_h, reflect, load_sem.at[9]),
+    ]
+    for copy in loads[:1] + index_loads + loads[1:] + panel_loads:
         copy.start()
 
     barrier = pltpu.get_barrier_semaphore()
@@ -147,8 +159,7 @@
             it, c, "fa", lambda s: face_out.at[it, s, group], lambda s: face_in.at[it, s, group],
             fa_send, fa_recv, "axial", before, after)
 
-    loads[0].wait()
-    for c in range(NCH):
+    def begin(c):
         for fl in range(FC):
             f = c * FC + fl
             for a in range(CA):
@@ -163,6 +174,11 @@
             side_out[0, side, c] = fixed(pack_f[side], LEVELS / BOUND)
         send_sides(0, c)
         send_faces(0, c)
+
+    loads[0].wait()
+    begin(0)
+    for copy in index_loads:
+        copy.wait()
 
     live_count = counts[0, 0]
     lane = lax.broadcasted_iota(jnp.int32, (1, RAD), 1)
@@ -223,6 +239,9 @@
         copy.start()
         q_a.append(copy)
 
+    for c in range(1, NCH):
+        begin(c)
+
     for copy in loads[1:]:
         copy.wait()
 
@@ -330,21 +349,26 @@
                 face_out[it + 1, end, f] = fixed(dirs[it + 1, f, a + 1, 8:24, :], inverse)
         send_faces(it + 1, c)
 
-    radp[...] = jnp.zeros((RAD, RAD), jnp.float32)
-    radp[0:PSLOT, :] = rad[...].astype(jnp.float32)
     for copy in q_a:
         copy.wait_recv()
-    ask_b[xy_pos] = ask_a[:, xy_pos]
+    for q in range(XY):
+        ask_t[q] = ask_a[:, q]
+    ask_b[xy_pos] = ask_t[xy_pos]
     q_b = []
     for k in range(1, XY):
         q, dev = xy_peer(k)
         copy = pltpu.make_async_remote_copy(
-            ask_a.at[:, q], ask_b.at[xy_pos], qb_send.at[k], qb_recv.at[k],
+            ask_t.at[q], ask_b.at[xy_pos], qb_send.at[k], qb_recv.at[k],
             device_id={"axial": dev}, device_id_type=MESH)
         copy.start()
         q_b.append(copy)
 
     interior(0)
+    finish(0, 0)
+    for copy in panel_loads:
+        copy.wait()
+    radp[...] = jnp.zeros((RAD, RAD), jnp.float32)
+    radp[0:PSLOT, :] = rad[...].astype(jnp.float32)
     for copy in q_b:
         copy.wait_recv()
 
@@ -370,7 +394,7 @@
         copy.start()
         p_a.append(copy)
 
-    for c in range(NCH):
+    for c in range(1, NCH):
         finish(0, c)
     interior(1)
 
@@ -425,6 +449,18 @@
             copy.wait_send()
 
 
+def deliver(x, r, rad, x_out, r_out, rad_out, sem):
+    copies = [
+        pltpu.make_async_copy(x, x_out, sem.at[0]),
+        pltpu.make_async_copy(r, r_out, sem.at[1]),
+        pltpu.make_async_copy(rad, rad_out, sem.at[2]),
+    ]
+    for copy in copies:
+        copy.start()
+    for copy in copies:
+        copy.wait()
+
+
 def body(
     source, storage, materials, conductance, mixing, counts, vis_owner, vis_slot, vis_block,
     radiosity_old, view_blocks, emission, reflect,
@@ -441,7 +477,7 @@
             pltpu.VMEM((NF, CA, CZ, CR), f32),
             pltpu.VMEM((PSLOT, RAD), f32),
         ),
-        in_specs=[anywhere, anywhere, anywhere, sm, sm, sm, vm, vm, vm, vm, vm, vm, vm],
+        in_specs=[anywhere, anywhere, anywhere, sm, sm, sm] + [anywhere] * 7,
         out_specs=(vm, vm, vm),
         scratch_shapes=[
             pltpu.VMEM((ITERS, NF, CA + 2, CZ + 16, CR), f32),
@@ -467,7 +503,15 @@
             pltpu.VMEM((RAD, RAD), f32),
             pltpu.VMEM((24, RAD), i32),
             pltpu.VMEM((RAD, RAD), f32),
-            dma((3,)),
+            pltpu.VMEM((VIS, PSLOT), i32),
+            pltpu.VMEM((VIS, PSLOT), i32),
+            pltpu.VMEM((VIS, PSLOT), i32),
+            pltpu.VMEM((PSLOT, RAD), b16),
+            pltpu.VMEM((NB, RAD, RAD), b16),
+            pltpu.VMEM((PSLOT, RAD), f32),
+            pltpu.VMEM((PSLOT, RAD), f32),
+            pltpu.VMEM((XY, ZN, 1, RAD), i32),
+            dma((10,)),
             *[dma((ITERS, NCH, 2)) for _ in range(8)],
             dma((ZN,)), dma((ZN,)), dma((XY,)), dma((XY,)),
             dma((XY,)), dma((XY,)), dma((ZN,)), dma((ZN,)),
@@ -479,6 +523,17 @@
         vis_owner[0, 0].T, vis_slot[0, 0].T, vis_block[0, 0].T,
         radiosity_old[0, 0], view_blocks, emission[0, 0], reflect[0, 0],
     )
+    x, r, rad = pl.pallas_call(
+        deliver,
+        out_shape=(
+            jax.ShapeDtypeStruct((NF, CA, CZ, CR), f32),
+            jax.ShapeDtypeStruct((NF, CA, CZ, CR), f32),
+            jax.ShapeDtypeStruct((PSLOT, RAD), f32),
+        ),
+        in_specs=[vm, vm, vm],
+        out_specs=(anywhere, anywhere, anywhere),
+        scratch_shapes=[dma((3,))],
+    )(*(pltpu.with_memory_space_constraint(part, pltpu.VMEM) for part in (x, r, rad)))
     return x, r, rad[None, None]
 
 

time: 53.1 us -> 50.1 us (0.944)
  the two profiles are of different devices: /device:TPU:24 before, /device:TPU:16 now
where the time goes in v3:
time: 50.1 us; the launch traced here: 49.8 us
  Pallas kernels  48.6 us (97%)
  between operations  1.29 us (3%)
    pallas_call x1, Pallas kernels, body(): pl.pallas_call(kernel, out_shape=(pltpu.VMEM((NF, CA, CZ, CR), f32), pltp...  47.4 us
    pallas_call x1, Pallas kernels, body(): pl.pallas_call(deliver, out_shape=(jax.ShapeDtypeStruct((NF, CA, CZ, CR),...  1.17 us

profile of v3, /device:TPU:16, one launch (start us, length us, event | category | flops | bytes accessed | tf_op | source)
XLA Modules:
  0.0 49.8 jit_solution(14113665530005392720)
XLA Ops:
  1.3 47.4 %shard_map.148 = (f32[12,4,16,256]{3,2,1,0:T(8,128)S(1)}, f32[12,4,16,256]{3,2,1,0:T(8,128)S(1)}, f32[120,128]{1,0:T(8,128)S(1)}) custom-call(f32[12,4,16,256]{3,2,1,0:T(8,128)} %source.1, f32[12,4,16,256]{3,2,1,0:T(8,128)} %storage.1, s32[4,16,256]{2,1,0:T(8,128)} %materials.1, f32[12]{0:T(128)} %cond.1, f32[12,4,12]{2,1,0:T(4,128)} %bitcast.17, ...), custom_call_target="tpu_custom_call" | custom-call | tf_op jit(solution)/shard_map/pallas_call | solution.py:473
  48.7 1.2 %shard_map.149 = (f32[12,4,16,256]{3,2,1,0:T(8,128)}, f32[12,4,16,256]{3,2,1,0:T(8,128)}, f32[120,128]{1,0:T(8,128)}) custom-call(f32[12,4,16,256]{3,2,1,0:T(8,128)S(1)} %get-tuple-element.9.x, f32[12,4,16,256]{3,2,1,0:T(8,128)S(1)} %get-tuple-element.10.r, f32[120,128]{1,0:T(8,128)S(1)} %get-tuple-element.11.rad), custom_call_target="tpu_custom_call" | custom-call | tf_op jit(solution)/shard_map/pallas_call | solution.py:526

commit v4 on v3

--- a/solution.py
+++ b/solution.py
@@ -25,6 +25,7 @@
 XY = XN * YN
 CAP = 5
 ROWS = 8
+PAIRS = 3
 NCH = 3
 FC = NF // NCH
 BOUND = 24.0
@@ -120,63 +121,6 @@
             dirs[it, f, 0, 8:24, :] = jnp.zeros((CZ, CR), jnp.float32)
             dirs[it, f, CA + 1, 8:24, :] = jnp.zeros((CZ, CR), jnp.float32)
 
-    pl.semaphore_wait(barrier, 4 + (ZN - 1) + (XY - 1))
-
-    def fixed(values, inverse):
-        return jnp.round(values * inverse).astype(jnp.int32).astype(jnp.int16)
-
-    def wide(coded):
-        return coded.astype(jnp.int32).astype(jnp.float32)
-
-    halos = {}
-
-    def send_pair(it, c, key, out, into, send, recv, axis, low, high):
-        pair = []
-        for side, dev in ((0, low), (1, high)):
-            copy = pltpu.make_async_remote_copy(
-                out(side), into(1 - side), send.at[it, c, side], recv.at[it, c, 1 - side],
-                device_id={axis: dev}, device_id_type=MESH)
-            copy.start()
-            pair.append(copy)
-        halos[key, it, c] = pair
-
-    def send_sides(it, c):
-        if it > 0:
-            send_pair(
-                it, c, "ss", lambda s: sscale_out.at[it, s, c], lambda s: sscale_in.at[it, s, c],
-                ss_send, ss_recv, "azim", left, right)
-        send_pair(
-            it, c, "sa", lambda s: side_out.at[it, s, c], lambda s: side_in.at[it, s, c],
-            sa_send, sa_recv, "azim", left, right)
-
-    def send_faces(it, c):
-        group = pl.ds(c * FC, FC)
-        if it > 0:
-            send_pair(
-                it, c, "fs", lambda s: fscale_out.at[it, s, c], lambda s: fscale_in.at[it, s, c],
-                fs_send, fs_recv, "axial", before, after)
-        send_pair(
-            it, c, "fa", lambda s: face_out.at[it, s, group], lambda s: face_in.at[it, s, group],
-            fa_send, fa_recv, "axial", before, after)
-
-    def begin(c):
-        for fl in range(FC):
-            f = c * FC + fl
-            for a in range(CA):
-                value = r_out[f, a]
-                dirs[0, f, a + 1, 8:24, :] = value * (1.0 / center_value)
-                row = fl * CA + a
-                pack_f[0, row : row + 1, :] = value[0:1, :]
-                pack_f[1, row : row + 1, :] = value[CZ - 1 : CZ, :]
-                if a in (0, CA - 1):
-                    face_out[0, a // (CA - 1), f] = fixed(value, LEVELS / BOUND)
-        for side in range(2):
-            side_out[0, side, c] = fixed(pack_f[side], LEVELS / BOUND)
-        send_sides(0, c)
-        send_faces(0, c)
-
-    loads[0].wait()
-    begin(0)
     for copy in index_loads:
         copy.wait()
 
@@ -206,7 +150,10 @@
             + (t >= 2 * ZN).astype(jnp.int32)
             + (t >= 3 * ZN).astype(jnp.int32)
         )
-        place = (t - ZN * x_of) * XY + x_of * YN + y_of
+        z_of = t - ZN * x_of
+        xy_of = x_of * YN + y_of
+        place = z_of * XY + xy_of
+        shelf = (xy_of * ZN + z_of) * 2 * PAIRS
         place = jnp.where(live, place, -1)
         hit = (sub96 == place).astype(jnp.float32)
         hit_b = hit.astype(jnp.bfloat16)
@@ -218,7 +165,7 @@
         hits.append(hit)
         ranks.append(rank)
         mine = jnp.sum(hit * rank, axis=0, keepdims=True)
-        tcol[k : k + 1, :] = place.astype(jnp.float32) * ROWS + mine
+        tcol[k : k + 1, :] = jnp.where(live, shelf, -ROWS).astype(jnp.float32) + mine
         tcol[8 + k : 9 + k, :] = idx[16 + k : 17 + k, :].astype(jnp.float32)
     asked = jnp.full((N_AXIAL, RAD), -1, jnp.int32)
     for r in range(CAP):
@@ -228,6 +175,61 @@
             total = total + jnp.where(ranks[k] == float(r), hits[k] * wanted, 0.0)
         value = jnp.sum(total, axis=1, keepdims=True).astype(jnp.int32) - 1
         asked = jnp.where(lane96 == r, value, asked)
+    pl.semaphore_wait(barrier, 4 + (ZN - 1) + (XY - 1))
+
+    def fixed(values, inverse):
+        return jnp.round(values * inverse).astype(jnp.int32).astype(jnp.int16)
+
+    def wide(coded):
+        return coded.astype(jnp.int32).astype(jnp.float32)
+
+    halos = {}
+
+    def send_pair(it, c, key, out, into, send, recv, axis, low, high):
+        pair = []
+        for side, dev in ((0, low), (1, high)):
+            copy = pltpu.make_async_remote_copy(
+                out(side), into(1 - side), send.at[it, c, side], recv.at[it, c, 1 - side],
+                device_id={axis: dev}, device_id_type=MESH)
+            copy.start()
+            pair.append(copy)
+        halos[key, it, c] = pair
+
+    def send_sides(it, c):
+        if it > 0:
+            send_pair(
+                it, c, "ss", lambda s: sscale_out.at[it, s, c], lambda s: sscale_in.at[it, s, c],
+                ss_send, ss_recv, "azim", left, right)
+        send_pair(
+            it, c, "sa", lambda s: side_out.at[it, s, c], lambda s: side_in.at[it, s, c],
+            sa_send, sa_recv, "azim", left, right)
+
+    def send_faces(it, c):
+        group = pl.ds(c * FC, FC)
+        if it > 0:
+            send_pair(
+                it, c, "fs", lambda s: fscale_out.at[it, s, c], lambda s: fscale_in.at[it, s, c],
+                fs_send, fs_recv, "axial", before, after)
+        send_pair(
+            it, c, "fa", lambda s: face_out.at[it, s, group], lambda s: face_in.at[it, s, group],
+            fa_send, fa_recv, "axial", before, after)
+
+    def begin(c):
+        for fl in range(FC):
+            f = c * FC + fl
+            for a in range(CA):
+                value = r_out[f, a]
+                dirs[0, f, a + 1, 8:24, :] = value * (1.0 / center_value)
+                row = fl * CA + a
+                pack_f[0, row : row + 1, :] = value[0:1, :]
+                pack_f[1, row : row + 1, :] = value[CZ - 1 : CZ, :]
+                if a in (0, CA - 1):
+                    face_out[0, a // (CA - 1), f] = fixed(value, LEVELS / BOUND)
+        for side in range(2):
+            side_out[0, side, c] = fixed(pack_f[side], LEVELS / BOUND)
+        send_sides(0, c)
+        send_faces(0, c)
+
     ask[...] = asked.reshape(ZN, XY, 1, RAD)
     ask_a[z_pos] = ask[z_pos]
     q_a = []
@@ -239,6 +241,8 @@
         copy.start()
         q_a.append(copy)
 
+    loads[0].wait()
+    begin(0)
     for c in range(1, NCH):
         begin(c)
 
@@ -364,7 +368,8 @@
         q_b.append(copy)
 
     interior(0)
-    finish(0, 0)
+    for c in range(NCH):
+        finish(0, c)
     for copy in panel_loads:
         copy.wait()
     radp[...] = jnp.zeros((RAD, RAD), jnp.float32)
@@ -373,52 +378,58 @@
         copy.wait_recv()
 
     panels = radp[...].astype(jnp.bfloat16)
-    lane_r = lax.broadcasted_iota(jnp.int32, (ZN, ROWS, RAD), 2)
-    sub_r = lax.broadcasted_iota(jnp.int32, (ZN, ROWS, RAD), 1)
-    for q in range(XY):
-        wanted = jnp.broadcast_to(ask_b[q], (ZN, ROWS, RAD))
+    lane_r = lax.broadcasted_iota(jnp.int32, (XY, ROWS, RAD), 2)
+    sub_r = lax.broadcasted_iota(jnp.int32, (XY, ROWS, RAD), 1)
+    for z in range(ZN):
+        wanted = jnp.broadcast_to(ask_b[:, z], (XY, ROWS, RAD))
         column = jnp.sum(
             jnp.where(lane_r == sub_r, wanted, 0), axis=2, keepdims=True)
         hot = ((lane_r == column) & (sub_r < CAP)).astype(jnp.float32)
         got = jnp.dot(
-            hot.reshape(ZN * ROWS, RAD).astype(jnp.bfloat16), panels,
+            hot.reshape(XY * ROWS, RAD).astype(jnp.bfloat16), panels,
             preferred_element_type=jnp.float32)
-        rows_out[q] = got.reshape(ZN, ROWS, RAD).astype(jnp.bfloat16)
-    rows_a[xy_pos] = rows_out[xy_pos]
+        got = got.reshape(XY, ROWS, RAD)
+        for pair in range(PAIRS):
+            rows_out[z, :, pair] = got[:, 2 * pair : 2 * pair + 2, :].astype(jnp.bfloat16)
+    rows_a[z_pos] = rows_out[z_pos]
     p_a = []
+    for k in range(1, ZN):
+        z, dev = z_peer(k)
+        copy = pltpu.make_async_remote_copy(
+            rows_out.at[z], rows_a.at[z_pos], pb_send.at[k], pb_recv.at[k],
+            device_id={"axial": dev}, device_id_type=MESH)
+        copy.start()
+        p_a.append(copy)
+
+    interior(1)
+    for c in range(NCH):
+        finish(1, c)
+    for copy in p_a:
+        copy.wait_recv()
+    rows_b[xy_pos] = rows_a[:, xy_pos]
+    p_b = []
     for k in range(1, XY):
         q, dev = xy_peer(k)
         copy = pltpu.make_async_remote_copy(
-            rows_out.at[q], rows_a.at[xy_pos], pa_send.at[k], pa_recv.at[k],
-            device_id={"axial": dev}, device_id_type=MESH)
-        copy.start()
-        p_a.append(copy)
-
-    for c in range(1, NCH):
-        finish(0, c)
-    interior(1)
-
-    for copy in p_a:
-        copy.wait_recv()
-    rows_b[z_pos] = rows_a[:, z_pos]
-    p_b = []
-    for k in range(1, ZN):
-        z, dev = z_peer(k)
-        copy = pltpu.make_async_remote_copy(
-            rows_a.at[:, z], rows_b.at[z_pos], pb_send.at[k], pb_recv.at[k],
+            rows_a.at[:, q], rows_b.at[xy_pos], pa_send.at[k], pa_recv.at[k],
             device_id={"axial": dev}, device_id_type=MESH)
         copy.start()
         p_b.append(copy)
 
+    interior(2)
+    early = [pair for (_, it, _), pair in halos.items() if it < ITERS - 1]
+    for group in early + [q_a, q_b, p_a]:
+        for copy in group:
+            copy.wait_send()
     for c in range(NCH):
-        finish(1, c)
-    interior(2)
+        finish(2, c)
+
 
     for copy in p_b:
         copy.wait_recv()
-    table = rows_b[...].astype(jnp.float32).reshape(N_AXIAL * ROWS, RAD).astype(jnp.bfloat16)
+    table = rows_b[...].astype(jnp.float32).reshape(N_AXIAL * 2 * PAIRS, RAD).astype(jnp.bfloat16)
     columns = jnp.transpose(tcol[...])
-    lane_t = lax.broadcasted_iota(jnp.int32, (RAD, N_AXIAL * ROWS), 1).astype(jnp.float32)
+    lane_t = lax.broadcasted_iota(jnp.int32, (RAD, N_AXIAL * 2 * PAIRS), 1).astype(jnp.float32)
     picked, kinds = [], []
     for k in range(VIS):
         pick = (lane_t == columns[:, k : k + 1]).astype(jnp.float32).astype(jnp.bfloat16)
@@ -441,10 +452,8 @@
     result = emission[...] * wall[0:PSLOT] + reflect[...] * incoming[0:PSLOT]
     rad_out[...] = jnp.where(slots < live_count, result, 0.0)
 
-    for c in range(NCH):
-        finish(2, c)
-
-    for group in list(halos.values()) + [q_a, q_b, p_a, p_b]:
+    late = [pair for (_, it, _), pair in halos.items() if it == ITERS - 1]
+    for group in late + [p_b]:
         for copy in group:
             copy.wait_send()
 
@@ -497,9 +506,9 @@
             pltpu.VMEM((ZN, XY, 1, RAD), i32),
             pltpu.VMEM((ZN, XY, 1, RAD), i32),
             pltpu.VMEM((XY, ZN, 1, RAD), i32),
-            pltpu.VMEM((XY, ZN, ROWS, RAD), b16),
-            pltpu.VMEM((XY, ZN, ROWS, RAD), b16),
-            pltpu.VMEM((ZN, XY, ROWS, RAD), b16),
+            pltpu.VMEM((ZN, XY, PAIRS, 2, RAD), b16),
+            pltpu.VMEM((ZN, XY, PAIRS, 2, RAD), b16),
+            pltpu.VMEM((XY, ZN, PAIRS, 2, RAD), b16),
             pltpu.VMEM((RAD, RAD), f32),
             pltpu.VMEM((24, RAD), i32),
             pltpu.VMEM((RAD, RAD), f32),

time: 50.1 us -> 48 us (0.958)
  the two profiles are of different devices: /device:TPU:16 before, /device:TPU:8 now
where the time goes in v4:
time: 48 us; the launch traced here: 47.7 us
  Pallas kernels  46.4 us (97%)
  between operations  1.29 us (3%)
    pallas_call x1, Pallas kernels, body(): pl.pallas_call(kernel, out_shape=(pltpu.VMEM((NF, CA, CZ, CR), f32), pltp...  45.3 us
    pallas_call x1, Pallas kernels, body(): pl.pallas_call(deliver, out_shape=(jax.ShapeDtypeStruct((NF, CA, CZ, CR),...  1.17 us

profile of v4, /device:TPU:8, one launch (start us, length us, event | category | flops | bytes accessed | tf_op | source)
XLA Modules:
  0.0 47.7 jit_solution(7919851687521812169)
XLA Ops:
  1.3 45.3 %shard_map.148 = (f32[12,4,16,256]{3,2,1,0:T(8,128)S(1)}, f32[12,4,16,256]{3,2,1,0:T(8,128)S(1)}, f32[120,128]{1,0:T(8,128)S(1)}) custom-call(f32[12,4,16,256]{3,2,1,0:T(8,128)} %source.1, f32[12,4,16,256]{3,2,1,0:T(8,128)} %storage.1, s32[4,16,256]{2,1,0:T(8,128)} %materials.1, f32[12]{0:T(128)} %cond.1, f32[12,4,12]{2,1,0:T(4,128)} %bitcast.17, ...), custom_call_target="tpu_custom_call" | custom-call | tf_op jit(solution)/shard_map/pallas_call | solution.py:482
  46.5 1.2 %shard_map.149 = (f32[12,4,16,256]{3,2,1,0:T(8,128)}, f32[12,4,16,256]{3,2,1,0:T(8,128)}, f32[120,128]{1,0:T(8,128)}) custom-call(f32[12,4,16,256]{3,2,1,0:T(8,128)S(1)} %get-tuple-element.9.x, f32[12,4,16,256]{3,2,1,0:T(8,128)S(1)} %get-tuple-element.10.r, f32[120,128]{1,0:T(8,128)S(1)} %get-tuple-element.11.rad), custom_call_target="tpu_custom_call" | custom-call | tf_op jit(solution)/shard_map/pallas_call | solution.py:535

commit v5 on v4

--- a/solution.py
+++ b/solution.py
@@ -26,7 +26,7 @@
 CAP = 5
 ROWS = 8
 PAIRS = 3
-NCH = 3
+NCH = 2
 FC = NF // NCH
 BOUND = 24.0
 LEVELS = 32760.0
@@ -246,6 +246,20 @@
     for c in range(1, NCH):
         begin(c)
 
+    for copy in q_a:
+        copy.wait_recv()
+    for q in range(XY):
+        ask_t[q] = ask_a[:, q]
+    ask_b[xy_pos] = ask_t[xy_pos]
+    q_b = []
+    for k in range(1, XY):
+        q, dev = xy_peer(k)
+        copy = pltpu.make_async_remote_copy(
+            ask_t.at[q], ask_b.at[xy_pos], qb_send.at[k], qb_recv.at[k],
+            device_id={"axial": dev}, device_id_type=MESH)
+        copy.start()
+        q_b.append(copy)
+
     for copy in loads[1:]:
         copy.wait()
 
@@ -268,12 +282,12 @@
     lane_c = lax.broadcasted_iota(jnp.int32, (8, CR), 1)
     row_c = lax.broadcasted_iota(jnp.int32, (CZ, CR), 0)
 
-    def interior(it):
+    def interior(it, fields):
         def body(a, carry):
             for h in range(2):
                 top = 8 + 8 * h
                 held = [dirs[it, g, a + 1, top : top + 8, :] for g in range(NF)]
-                for f in range(NF):
+                for f in fields:
                     acc = coef[f * NF, a, 8 * h : 8 * h + 8, :] * held[0]
                     for g in range(1, NF):
                         acc = acc + coef[f * NF + g, a, 8 * h : 8 * h + 8, :] * held[g]
@@ -353,22 +367,10 @@
                 face_out[it + 1, end, f] = fixed(dirs[it + 1, f, a + 1, 8:24, :], inverse)
         send_faces(it + 1, c)
 
-    for copy in q_a:
-        copy.wait_recv()
-    for q in range(XY):
-        ask_t[q] = ask_a[:, q]
-    ask_b[xy_pos] = ask_t[xy_pos]
-    q_b = []
-    for k in range(1, XY):
-        q, dev = xy_peer(k)
-        copy = pltpu.make_async_remote_copy(
-            ask_t.at[q], ask_b.at[xy_pos], qb_send.at[k], qb_recv.at[k],
-            device_id={"axial": dev}, device_id_type=MESH)
-        copy.start()
-        q_b.append(copy)
-
-    interior(0)
+    interior(0, range(FC))
     for c in range(NCH):
+        if c + 1 < NCH:
+            interior(0, range((c + 1) * FC, (c + 2) * FC))
         finish(0, c)
     for copy in panel_loads:
         copy.wait()
@@ -401,8 +403,10 @@
         copy.start()
         p_a.append(copy)
 
-    interior(1)
+    interior(1, range(FC))
     for c in range(NCH):
+        if c + 1 < NCH:
+            interior(1, range((c + 1) * FC, (c + 2) * FC))
         finish(1, c)
     for copy in p_a:
         copy.wait_recv()
@@ -416,7 +420,7 @@
         copy.start()
         p_b.append(copy)
 
-    interior(2)
+    interior(2, range(NF))
     early = [pair for (_, it, _), pair in halos.items() if it < ITERS - 1]
     for group in early + [q_a, q_b, p_a]:
         for copy in group:

time: 48 us -> 47.2 us (0.983)
  the two profiles are of different devices: /device:TPU:8 before, /device:TPU:17 now
where the time goes in v5:
time: 47.2 us; the launch traced here: 47 us
  Pallas kernels  45.7 us (97%)
  between operations  1.29 us (3%)
    pallas_call x1, Pallas kernels, body(): pl.pallas_call(kernel, out_shape=(pltpu.VMEM((NF, CA, CZ, CR), f32), pltp...  44.5 us
    pallas_call x1, Pallas kernels, body(): pl.pallas_call(deliver, out_shape=(jax.ShapeDtypeStruct((NF, CA, CZ, CR),...  1.17 us

profile of v5, /device:TPU:17, one launch (start us, length us, event | category | flops | bytes accessed | tf_op | source)
XLA Modules:
  0.0 47.0 jit_solution(3689395017438637411)
XLA Ops:
  1.3 44.5 %shard_map.148 = (f32[12,4,16,256]{3,2,1,0:T(8,128)S(1)}, f32[12,4,16,256]{3,2,1,0:T(8,128)S(1)}, f32[120,128]{1,0:T(8,128)S(1)}) custom-call(f32[12,4,16,256]{3,2,1,0:T(8,128)} %source.1, f32[12,4,16,256]{3,2,1,0:T(8,128)} %storage.1, s32[4,16,256]{2,1,0:T(8,128)} %materials.1, f32[12]{0:T(128)} %cond.1, f32[12,4,12]{2,1,0:T(4,128)} %bitcast.17, ...), custom_call_target="tpu_custom_call" | custom-call | tf_op jit(solution)/shard_map/pallas_call | solution.py:486
  45.8 1.2 %shard_map.149 = (f32[12,4,16,256]{3,2,1,0:T(8,128)}, f32[12,4,16,256]{3,2,1,0:T(8,128)}, f32[120,128]{1,0:T(8,128)}) custom-call(f32[12,4,16,256]{3,2,1,0:T(8,128)S(1)} %get-tuple-element.9.x, f32[12,4,16,256]{3,2,1,0:T(8,128)S(1)} %get-tuple-element.10.r, f32[120,128]{1,0:T(8,128)S(1)} %get-tuple-element.11.rad), custom_call_target="tpu_custom_call" | custom-call | tf_op jit(solution)/shard_map/pallas_call | solution.py:539
